TPU v7x, 256 devices: a whole 4x4x8 slice. The times are simulated.
256 devices in a mesh: cluster: 16 (over z_lo, x), narrow: 16 (over y, z_hi, core).
Axes of the slice: x: 4, y: 4, z: 8 (z_hi: 2, z_lo: 4; z = z_hi * 4 + z_lo), core: 2. Of those that a mesh axis runs over, the one named last changes fastest.
Arguments:
- edge_feats: bfloat16 [524288, 512], P(('cluster', 'narrow')), may hold values from -6 to 6
- cotangent: bfloat16 [524288, 512], P(('cluster', 'narrow')), may hold values from -6 to 6
- down_weight: bfloat16 [512, 64], replicated, may hold values from -0.25 to 0.25
- up_weight: bfloat16 [64, 512], replicated, may hold values from -0.75 to 0.75
- inner_weight: bfloat16 [1, 512, 512], replicated, may hold values from -0.25 to 0.25
- outer_weight: bfloat16 [1, 512, 512], replicated, may hold values from -0.25 to 0.25
- angular: bfloat16 [8192, 8, 4096], P(('cluster', 'narrow')), may hold values from -0.375 to 0.375
- reverse: int32 [524288], P(('cluster', 'narrow')), may hold values from 0 to 524287, as said below
- sources: int32 [8192, 8], P(('cluster', 'narrow')), may hold values from 0 to 8191, as said below
- counts: int32 [8192], P(('cluster', 'narrow')), may hold values from 1 to 8
Outputs:
- output: bfloat16 [524288, 512], P(('cluster', 'narrow'))
- grad_x: bfloat16 [524288, 512], P(('cluster', 'narrow'))
Inputs may be any that keep to these rules, and one draw needn't show every extreme that they name: reverse is an involution without fixed points, and reverse[e] // 2048 == ((e + 262144) % 524288) // 2048. sources[k, s] // 512 == k // 512; among the slots of the blocks of one device (blocks m * 32 to (m + 1) * 32 - 1), exactly 16 name a block j with (j % 512) // 32 == i, for every i below 16; slots s >= counts[k] hold valid block numbers that are not used.
All inputs are finite; a program needn't handle non-finite values.
Results may differ from a plain program's by a relative error of at most 0.0075.
Values may be sent and summed in bfloat16 or wider, within the bound.
A program may use at most 128 MiB of HBM per device.

v0:
```python
import jax
import jax.numpy as jnp
from jax import lax
from jax.sharding import PartitionSpec as P

ROOT_HALF = 0.7071067811865476


def swapped(array, axis, bit):
    return lax.ppermute(array, axis, [(i, i ^ 1 << bit) for i in range(lax.axis_size(axis))])


def side_by_side(arrays, axis, split_dim, concat_dim, along):
    columns = [a.reshape(*a.shape[:along], -1) for a in arrays]
    both = jnp.concatenate(columns, axis=along)
    result, at, done = (
        lax.all_to_all(both, axis, split_axis=split_dim, concat_axis=concat_dim, tiled=True),
        0,
        [],
    )
    for a, column in zip(arrays, columns):
        slab = result[..., at : at + column.shape[along]]
        done.append(slab.reshape(*slab.shape[:along], *a.shape[along:]))
        at += column.shape[along]
    return tuple(done)


def silu_grad(pre_act):
    squash = jax.nn.sigmoid(pre_act)
    return squash * (1.0 + pre_act * (1.0 - squash))


def dot_trans(operand, matrix):
    return lax.dot_general(
        operand, matrix, (((1,), (1,)), ((), ())), preferred_element_type=jnp.float32
    )


def split_parts(values):
    high_part = values.astype(jnp.bfloat16)
    low_part = (values - high_part.astype(jnp.float32)).astype(jnp.bfloat16)
    return (high_part, low_part)


def on_device(
    edge_feats,
    cotangent,
    down_weight,
    up_weight,
    inner_weight,
    outer_weight,
    angular,
    reverse,
    sources,
    counts,
):
    lane_count = lax.axis_size("narrow")
    top_bit = lax.axis_size("cluster").bit_length() - 2
    local_blocks = counts.shape[0]
    local_edges = edge_feats.shape[0]
    block_edges = local_edges // local_blocks
    trip_width = down_weight.shape[1]
    slot_count = sources.shape[1]
    cluster_blocks = local_blocks * lane_count
    source_local = sources % cluster_blocks
    live_mask = lax.broadcasted_iota(jnp.int32, sources.shape, 1) < counts[:, None]
    rev_slot = reverse % local_edges
    angle_mats = angular.reshape(local_blocks, slot_count, block_edges, block_edges)
    pre_down = jnp.dot(edge_feats, down_weight, preferred_element_type=jnp.float32)
    trip_feat = jax.nn.silu(pre_down).astype(jnp.bfloat16)
    trip_blocks = trip_feat.reshape(local_blocks, block_edges * trip_width)
    shard_piece = lax.all_gather(trip_blocks, "narrow", axis=0, tiled=True)
    columns = lax.broadcasted_iota(jnp.int32, (1, 1, shard_piece.shape[0]), 2)
    selector = ((source_local[:, :, None] == columns) & live_mask[:, :, None]).astype(jnp.bfloat16)
    picked = jnp.einsum("ksp,pf->ksf", selector, shard_piece, preferred_element_type=jnp.float32)
    picked = picked.astype(jnp.bfloat16).reshape(local_blocks, slot_count, block_edges, trip_width)
    trip_sum = jnp.einsum("ksij,ksjf->kif", angle_mats, picked, preferred_element_type=jnp.float32)
    trip_round = trip_sum.reshape(local_edges, trip_width).astype(jnp.bfloat16)
    pre_up = jnp.dot(trip_round, up_weight, preferred_element_type=jnp.float32)
    up_feat = jax.nn.silu(pre_up).astype(jnp.bfloat16)
    partner_trip = swapped(trip_round, "cluster", top_bit)
    partner_pre = jnp.dot(partner_trip[rev_slot], up_weight, preferred_element_type=jnp.float32)
    partner_up = jax.nn.silu(partner_pre).astype(jnp.bfloat16)
    message = (up_feat.astype(jnp.float32) + partner_up.astype(jnp.float32)) * ROOT_HALF
    hidden_state = (edge_feats.astype(jnp.float32) + message) * ROOT_HALF
    layer_index = 0
    state_round = hidden_state.astype(jnp.bfloat16)
    pre_in = jnp.dot(state_round, inner_weight[layer_index], preferred_element_type=jnp.float32)
    act_feat = jax.nn.silu(pre_in).astype(jnp.bfloat16)
    pre_out = jnp.dot(act_feat, outer_weight[layer_index], preferred_element_type=jnp.float32)
    saved_acts = [(pre_in, pre_out)]
    hidden_state = (hidden_state + jax.nn.silu(pre_out)) * ROOT_HALF
    output = hidden_state.astype(jnp.bfloat16)
    grad_state = cotangent.astype(jnp.float32)
    for layer_index in reversed(range(inner_weight.shape[0])):
        pre_in, pre_out = saved_acts[layer_index]
        grad_state = grad_state * ROOT_HALF
        grad_out = (grad_state * silu_grad(pre_out)).astype(jnp.bfloat16)
        grad_act = dot_trans(grad_out, outer_weight[layer_index])
        grad_in = (grad_act * silu_grad(pre_in)).astype(jnp.bfloat16)
        grad_state = grad_state + dot_trans(grad_in, inner_weight[layer_index])
    grad_msg = grad_state * ROOT_HALF
    grad_msg_round = grad_msg.astype(jnp.bfloat16)
    partner_grad = swapped(grad_msg_round, "cluster", top_bit)[rev_slot]
    grad_up = (grad_msg + partner_grad.astype(jnp.float32)) * ROOT_HALF
    grad_pre_up = (grad_up * silu_grad(pre_up)).astype(jnp.bfloat16)
    grad_trip = dot_trans(grad_pre_up, up_weight).astype(jnp.bfloat16)
    grad_blocks = grad_trip.reshape(local_blocks, block_edges, trip_width)
    pair_terms = jnp.einsum(
        "ksij,kif->ksjf", angle_mats, grad_blocks, preferred_element_type=jnp.float32
    )
    pair_terms = pair_terms.reshape(local_blocks, slot_count, block_edges * trip_width)
    slot_total = local_blocks * slot_count
    quota = slot_total // lane_count
    flat_terms = (pair_terms * live_mask[:, :, None].astype(jnp.float32)).reshape(
        slot_total, block_edges * trip_width
    )
    owner_lane = (source_local // local_blocks).reshape(slot_total)
    order = jnp.argsort(owner_lane, stable=True)
    sent_terms = flat_terms[order].reshape(lane_count, quota, block_edges * trip_width)
    sent_ids = (
        (source_local % local_blocks)
        .reshape(slot_total)[order]
        .astype(jnp.float32)
        .reshape(lane_count, quota)
    )
    got_terms, got_ids = tuple(
        (
            part.astype(jnp.float32)
            for part in side_by_side(
                (sent_terms.astype(jnp.bfloat16), sent_ids.astype(jnp.bfloat16)), "narrow", 0, 0, 2
            )
        )
    )
    got_terms = got_terms.reshape(slot_total, block_edges * trip_width)
    got_ids = got_ids.reshape(1, slot_total).astype(jnp.int32)
    selector = (lax.broadcasted_iota(jnp.int32, (local_blocks, 1), 0) == got_ids).astype(
        jnp.bfloat16
    )
    high_part, low_part = split_parts(got_terms)
    source_grad = jnp.dot(selector, high_part, preferred_element_type=jnp.float32) + jnp.dot(
        selector, low_part, preferred_element_type=jnp.float32
    )
    source_grad = source_grad.reshape(local_edges, trip_width)
    grad_pre_down = (source_grad * silu_grad(pre_down)).astype(jnp.bfloat16)
    grad_x = grad_msg + dot_trans(grad_pre_down, down_weight)
    return (output, grad_x.astype(jnp.bfloat16))


def solution(mesh):
    in_specs = (
        P(("cluster", "narrow"), None),
        P(("cluster", "narrow"), None),
        P(),
        P(),
        P(),
        P(),
        P(("cluster", "narrow"), None, None),
        P(("cluster", "narrow")),
        P(("cluster", "narrow"), None),
        P(("cluster", "narrow")),
    )
    out_specs = (P(("cluster", "narrow"), None), P(("cluster", "narrow"), None))
    return jax.shard_map(
        on_device, mesh=mesh, in_specs=in_specs, out_specs=out_specs, check_vma=False
    )
```

profile of v0, /device:TPU:1, one launch (start us, length us, event | category | flops | bytes accessed | tf_op | source)
XLA Modules:
  0.0 369.6 jit_solution(938213742691070242)
XLA Ops:
  7.2 0.0 copy-start
  7.2 0.0 copy-start.9
  7.2 0.0 copy-start.3
  7.2 0.0 all-gather.2.cloned.1.call-start
  7.2 3.3 multiply_convert_fusion.13
  10.6 0.3 copy.27
  10.8 1.2 reshape.110
  12.0 0.0 all-gather.2.cloned.1.call-update
  12.0 0.0 copy-done.9
  12.1 0.1 copy.26
  12.2 0.0 copy-done.3
  12.2 5.5 %reshape.112 = bf16[32,8,64,64]{3,2,1,0:T(8,128)(2,1)} reshape(bf16[32,8,4096]{2,1,0:T(8,128)(2,1)S(1)} %copy-done.3) | data formatting | bytes 4194304 | tf_op jit(solution)/shard_map/reshape | solution.py:68
  17.7 0.0 copy-done.8
  17.7 0.0 copy-done.10
  17.7 0.1 fusion.34
  17.8 75.6 %all-gather.2.cloned.1.call-done = bf16[512,4096]{1,0:T(8,128)(2,1)} async-done(((bf16[32,4096]{1,0:T(8,128)(2,1)}), bf16[512,4096]{1,0:T(8,128)(2,1)}) %all-gather.2.cloned.1.call-update) | async-done | bytes 4194320 | tf_op jit(solution)/shard_map/all_gather | solution.py:72
  93.4 3.5 convolution_convert_fusion
  96.9 5.5 %reshape.111 = bf16[32,8,64,64]{3,2,1,0:T(8,128)(2,1)} reshape(bf16[32,8,4096]{2,1,0:T(8,128)(2,1)S(1)} %convolution_convert_fusion) | data formatting | bytes 4194304 | tf_op jit(solution)/shard_map/reshape | solution.py:76
  102.4 4.8 %fusion.6 = bf16[32,64,64]{1,2,0:T(8,128)(2,1)S(1)} fusion(bf16[32,8,64,64]{3,2,1,0:T(8,128)(2,1)} %reshape.111, bf16[32,8,64,64]{3,2,1,0:T(8,128)(2,1)} %reshape.112), kind=kOutput, calls=%fused_computation.32 | convolution fusion | flops 134348800 | bytes 4456448 | tf_op jit(solution)/shard_map/ksij,ksjf->kif/dot_general | solution.py:77
  107.2 0.3 copy.29
  107.6 0.5 convert_element_type.141
  108.0 0.3 copy.30
  108.3 0.7 collective-permute-start
  109.0 0.0 copy-done.6
  109.0 2.7 fusion.38
  111.7 22.8 %collective-permute-done = bf16[2048,64]{1,0:T(8,128)(2,1)S(1)} collective-permute-done((bf16[2048,64]{1,0:T(8,128)(2,1)S(1)}, bf16[2048,64]{1,0:T(8,128)(2,1)S(1)}, u32[]{:S(2)}, u32[]{:S(2)}) %collective-permute-start) | collective-permute-done | bytes 262176 | tf_op jit(solution)/shard_map/ppermute | solution.py:10
  134.5 6.2 %gather_fusion = bf16[2048,64]{1,0:T(8,128)(2,1)S(1)} fusion(bf16[2048,64]{1,0:T(8,128)(2,1)S(1)} %collective-permute-done, s32[2048]{0:T(1024)S(1)} %fusion.22), kind=kCustom, calls=%fused_computation | custom fusion | bytes 532480 | tf_op jit(solution)/shard_map/gather | solution.py:82
  140.6 0.0 copy-start.5
  140.7 4.5 %add_multiply_fusion.1 = f32[2048,512]{1,0:T(8,128)S(1)} fusion(bf16[2048,512]{1,0:T(8,128)(2,1)} %param.10, bf16[2048,64]{1,0:T(8,128)(2,1)S(1)} %gather_fusion, bf16[64,512]{1,0:T(8,128)(2,1)S(1)} %copy-done.6, f32[2048,512]{1,0:T(8,128)} %fusion.38), kind=kOutput, calls=%fused_computation.18 | convolution fusion | flops 152043520 | bytes 10813440 | tf_op jit(solution)/shard_map/dot_general | solution.py:82
  145.2 0.0 copy-done.5
  145.2 1.2 fusion.1
  146.5 4.0 %multiply_convert_fusion.3 = (bf16[2048,512]{1,0:T(8,128)(2,1)}, f32[2048,512]{1,0:T(8,128)}) fusion(f32[2048,512]{1,0:T(8,128)S(1)} %add_multiply_fusion.1, bf16[1,512,512]{2,1,0:T(8,128)(2,1)S(1)} %copy-done, f32[2048,512]{1,0:T(8,128)S(1)} %fusion.1), kind=kOutput, calls=%fused_computation.14 | convolution fusion | flops 1086324736 | bytes 15204352 | tf_op jit(solution)/shard_map/dot_general | solution.py:90
  150.5 10.1 %fusion.35 = (bf16[2048,512]{1,0:T(8,128)(2,1)}, f32[2048,512]{1,0:T(8,128)}) fusion(bf16[1,512,512]{2,1,0:T(8,128)(2,1)S(1)} %copy-done.5, f32[2048,512]{1,0:T(8,128)} %copy-done.2, f32[2048,512]{1,0:T(8,128)} %get-tuple-element.12, bf16[2048,512]{1,0:T(8,128)(2,1)} %param.11, bf16[1,512,512]{2,1,0:T(8,128)(2,1)S(1)} %copy-done), kind=kOutput, calls=%fused_computation.80 | convolution fusion | flops 2173698048 | bytes 17825792 | tf_op jit(solution)/shard_map/dot_general | solution.py:34
  160.5 0.0 collective-permute-start.1
  160.6 0.1 copy.34
  160.6 0.1 reshape.116
  160.7 0.1 copy.33
  160.8 0.1 reshape.115
  160.9 3.1 sort.17
  164.1 1.9 gather_fusion.3
  166.0 0.2 convert_element_type.170
  166.3 0.1 reshape.120
  166.3 85.4 %collective-permute-done.1 = bf16[2048,512]{1,0:T(8,128)(2,1)S(1)} collective-permute-done((bf16[2048,512]{1,0:T(8,128)(2,1)}, bf16[2048,512]{1,0:T(8,128)(2,1)S(1)}, u32[]{:S(2)}, u32[]{:S(2)}) %collective-permute-start.1) | collective-permute-done | bytes 2097184 | tf_op jit(solution)/shard_map/ppermute | solution.py:10
  251.7 9.2 %gather_fusion.1 = bf16[2048,512]{1,0:T(8,128)(2,1)} fusion(bf16[2048,512]{1,0:T(8,128)(2,1)S(1)} %collective-permute-done.1, s32[2048]{0:T(1024)S(1)} %fusion.22), kind=kCustom, calls=%fused_computation.1 | custom fusion | bytes 4202496 | tf_op jit(solution)/shard_map/gather | solution.py:104
  260.9 6.0 %convolution_convert_fusion.1 = bf16[2048,64]{0,1:T(8,128)(2,1)S(1)} fusion(bf16[64,512]{1,0:T(8,128)(2,1)S(1)} %copy-done.6, f32[2048,512]{1,0:T(8,128)} %fusion.38, f32[2048,512]{1,0:T(8,128)} %get-tuple-element.14, bf16[2048,512]{1,0:T(8,128)(2,1)} %gather_fusion.1), kind=kOutput, calls=%fused_computation.23 | convolution fusion | flops 146931712 | bytes 10813440 | tf_op jit(solution)/shard_map/dot_general | solution.py:34
  266.9 0.5 reshape.113
  267.5 6.6 %convolution_bitcast_fusion = f32[32,8,64,64]{2,3,1,0:T(8,128)} fusion(bf16[32,8,64,64]{3,2,1,0:T(8,128)(2,1)} %reshape.112, bf16[32,64,64,1]{1,0,2,3:T(8,128)(2,1)S(1)} %bitcast.55), kind=kOutput, calls=%fused_computation.22 | convolution fusion | flops 134217728 | bytes 6553600 | tf_op jit(solution)/shard_map/ksij,kif->ksjf/dot_general | solution.py:109
  274.1 9.0 %copy.32 = f32[32,8,64,64]{3,2,1,0:T(8,128)} copy(f32[32,8,64,64]{2,3,1,0:T(8,128)} %convolution_bitcast_fusion) | data formatting | bytes 8388608 | tf_op jit(solution)/shard_map/ksij,kif->ksjf/dot_general | solution.py:109
  283.1 7.9 %reshape.114 = f32[256,4096]{1,0:T(8,128)} reshape(f32[32,8,64,64]{3,2,1,0:T(8,128)} %copy.32) | data formatting | bytes 8388608 | tf_op jit(solution)/shard_map/reshape | solution.py:112
  291.0 2.6 broadcast_multiply_fusion
  293.6 3.2 gather_fusion.2
  296.8 1.8 pad_maximum_fusion
  298.6 57.4 %all_to_all.5 = bf16[16,16,4097]{2,1,0:T(8,128)(2,1)S(1)} all-to-all(bf16[16,16,4097]{2,1,0:T(8,128)(2,1)S(1)} %pad_maximum_fusion), channel_id=1, replica_groups=mesh['cluster'=16,'narrow'=16] {'narrow'}, dimensions={0} | all-to-all | bytes 4195328 | tf_op jit(solution)/shard_map/all_to_all | solution.py:17
  356.0 0.3 convert_reduce_fusion
  356.3 0.1 convert_element_type.165
  356.4 0.3 slice.17
  356.7 0.0 copy-start.7
  356.7 0.5 fusion.18
  357.2 0.5 convolution_add_fusion
  357.7 0.0 copy-start.1
  357.7 0.4 reshape.119
  358.1 0.3 copy.36
  358.5 4.3 %add_convert_fusion = bf16[2048,512]{1,0:T(8,128)(2,1)} fusion(f32[2048,512]{1,0:T(8,128)} %get-tuple-element.14, bf16[512,64]{0,1:T(8,128)(2,1)S(1)} %copy-done.7, f32[2048,64]{0,1:T(8,128)S(1)} %copy.36, f32[2048,64]{0,1:T(8,128)S(1)} %copy-done.4), kind=kOutput, calls=%fused_computation.7 | convolution fusion | flops 137494528 | bytes 7405568 | tf_op jit(solution)/shard_map/dot_general | solution.py:34
  362.7 0.0 copy-done.1
  (15 shorter events, 0.1 us)
Async XLA Ops:
  7.2 139.3 %copy-start = (bf16[1,512,512]{2,1,0:T(8,128)(2,1)S(1)}, bf16[1,512,512]{2,1,0:T(8,128)(2,1)}, u32[]{:S(2)}) copy-start(bf16[1,512,512]{2,1,0:T(8,128)(2,1)} %param.15) | copy-start | bytes 1572868
  7.2 4.9 %copy-start.9 = (s32[32,8]{0,1:T(8,128)S(1)}, s32[32,8]{0,1:T(8,128)}, u32[]{:S(2)}) copy-start(s32[32,8]{0,1:T(8,128)} %param.18) | copy-start | bytes 3076
  7.2 5.0 %copy-start.3 = (bf16[32,8,4096]{2,1,0:T(8,128)(2,1)S(1)}, bf16[32,8,4096]{2,1,0:T(8,128)(2,1)}, u32[]{:S(2)}) copy-start(bf16[32,8,4096]{2,1,0:T(8,128)(2,1)} %param.16) | copy-start | bytes 6291460
  7.2 86.2 %all-gather.2.cloned.1.call-start = ((), (), s32[]{:S(2)}) async-start(), calls=%async_computation.1 | async-start | bytes 4456448 | tf_op jit(solution)/shard_map/all_gather | solution.py:72
  10.6 7.1 %copy-start.8 = (s32[2048]{0:T(1024)S(1)}, s32[2048]{0:T(1024)}, u32[]{:S(2)}) copy-start(s32[2048]{0:T(1024)} %param.17) | copy-start | bytes 24580
  10.6 7.1 %copy-start.10 = (s32[32]{0:T(128)S(1)}, s32[32]{0:T(128)}, u32[]{:S(2)}) copy-start(s32[32]{0:T(128)} %param.19) | copy-start | bytes 388
  102.4 6.6 %copy-start.6 = (bf16[64,512]{1,0:T(8,128)(2,1)S(1)}, bf16[64,512]{1,0:T(8,128)(2,1)}, u32[]{:S(2)}) copy-start(bf16[64,512]{1,0:T(8,128)(2,1)} %param.13) | copy-start | bytes 196612
  108.3 26.1 %collective-permute-start = (bf16[2048,64]{1,0:T(8,128)(2,1)S(1)}, bf16[2048,64]{1,0:T(8,128)(2,1)S(1)}, u32[]{:S(2)}, u32[]{:S(2)}) collective-permute-start(bf16[2048,64]{1,0:T(8,128)(2,1)S(1)} %copy.30), channel_id=1, source_target_pairs={{0,128},{16,144},{32,160},{48,176},{64,192},{80,208},{96,224},{112... | collective-permute-start | bytes 786440 | tf_op jit(solution)/shard_map/ppermute | solution.py:10
  140.6 4.5 %copy-start.5 = (bf16[1,512,512]{2,1,0:T(8,128)(2,1)S(1)}, bf16[1,512,512]{2,1,0:T(8,128)(2,1)}, u32[]{:S(2)}) copy-start(bf16[1,512,512]{2,1,0:T(8,128)(2,1)} %param.14) | copy-start | bytes 1572868
  146.5 4.0 %copy-start.2 = (f32[2048,512]{1,0:T(8,128)}, f32[2048,512]{1,0:T(8,128)S(1)}, u32[]{:S(2)}) copy-start(f32[2048,512]{1,0:T(8,128)S(1)} %fusion.1) | copy-start | bytes 12582916
  160.5 91.2 %collective-permute-start.1 = (bf16[2048,512]{1,0:T(8,128)(2,1)}, bf16[2048,512]{1,0:T(8,128)(2,1)S(1)}, u32[]{:S(2)}, u32[]{:S(2)}) collective-permute-start(bf16[2048,512]{1,0:T(8,128)(2,1)} %get-tuple-element.13), channel_id=1, source_target_pairs={{0,128},{16,144},{32,160},{48,176},{64,192},{80,208},{96,224},{112... | collective-permute-start | bytes 6291464 | tf_op jit(solution)/shard_map/ppermute | solution.py:10
  356.7 1.8 copy-start.4
  356.7 1.8 copy-start.7
  357.7 5.0 %copy-start.1 = (bf16[1,512,512]{2,1,0:T(8,128)(2,1)S(1)}, bf16[1,512,512]{2,1,0:T(8,128)(2,1)}, u32[]{:S(2)}) copy-start(bf16[1,512,512]{2,1,0:T(8,128)(2,1)} %param.15) | copy-start | bytes 1572868
Sparse Core Ops, SparseCore 0:
  12.2 81.2 all-gather.1
where the time goes:
time: 370 us
  waiting for transfers between devices  184 us (50%)
  blocking collectives  57.4 us (16%)
  local copies, waits for them, and re-layouts  53.4 us (14%)
  matrix products  52 us (14%)
  between operations  14.3 us (4%)
  other arithmetic  8.01 us (2%)
    ppermute x2, waiting for transfers between devices, swapped(): lax.ppermute(array, axis, [(i, i ^ 1 << bit) for i in range(lax.axis_size...  108 us
    all_gather x1, waiting for transfers between devices, on_device(): shard_piece = lax.all_gather(trip_blocks, 'narrow', axis=0, tiled=True)  75.6 us
    all_to_all x1, blocking collectives, side_by_side(): lax.all_to_all(both, axis, split_axis=split_dim, concat_axis=concat_dim,...  57.4 us
    dot_general x3, matrix products, dot_trans(): lax.dot_general(operand, matrix, (((1,), (1,)), ((), ())), preferred_elem...  20.3 us
    gather x1, local copies, waits for them, and re-layouts, on_device(): partner_grad = swapped(grad_msg_round, 'cluster', top_bit)[rev_slot]  9.2 us
    dot_general x1, local copies, waits for them, and re-layouts, on_device(): jnp.einsum('ksij,kif->ksjf', angle_mats, grad_blocks, preferred_element_t...  8.99 us
    reshape x1, local copies, waits for them, and re-layouts, on_device(): pair_terms.reshape(local_blocks, slot_count, block_edges * trip_width)  7.9 us
  transfers between devices with their start and end apart: 3, of which 3 were waited for; matrix products, arithmetic and copies ran while one was open for 4% of the time, Pallas kernels for 0%

commit v1 on v0

--- a/solution.py
+++ b/solution.py
@@ -101,10 +101,13 @@
         grad_state = grad_state + dot_trans(grad_in, inner_weight[layer_index])
     grad_msg = grad_state * ROOT_HALF
     grad_msg_round = grad_msg.astype(jnp.bfloat16)
-    partner_grad = swapped(grad_msg_round, "cluster", top_bit)[rev_slot]
-    grad_up = (grad_msg + partner_grad.astype(jnp.float32)) * ROOT_HALF
-    grad_pre_up = (grad_up * silu_grad(pre_up)).astype(jnp.bfloat16)
-    grad_trip = dot_trans(grad_pre_up, up_weight).astype(jnp.bfloat16)
+    partner_part = (
+        grad_msg_round.astype(jnp.float32) * ROOT_HALF * silu_grad(partner_pre)
+    ).astype(jnp.bfloat16)
+    sent_part = dot_trans(partner_part, up_weight).astype(jnp.bfloat16)
+    got_part = swapped(sent_part, "cluster", top_bit)[rev_slot]
+    own_part = (grad_msg * ROOT_HALF * silu_grad(pre_up)).astype(jnp.bfloat16)
+    grad_trip = (dot_trans(own_part, up_weight) + got_part.astype(jnp.float32)).astype(jnp.bfloat16)
     grad_blocks = grad_trip.reshape(local_blocks, block_edges, trip_width)
     pair_terms = jnp.einsum(
         "ksij,kif->ksjf", angle_mats, grad_blocks, preferred_element_type=jnp.float32

time: 370 us -> 291 us (0.79)
  waiting for transfers between devices: 184 us -> 103 us
    ppermute x2, waiting for transfers between devices: 108 us -> 32.9 us  [swapped(): lax.ppermute(array, axis, [(i, i ^ 1 << bit) for i in range(lax.axis_size...]
    all_gather x1, waiting for transfers between devices: 75.6 us -> 69.8 us  [on_device(): shard_piece = lax.all_gather(trip_blocks, 'narrow', axis=0, tiled=True)]
    dot_general x1, matrix products: 4.53 us -> 0.67 us  [on_device(): jnp.dot(partner_trip[rev_slot], up_weight, preferred_element_type=jnp.flo...]
    gather x1 -> x2, local copies, waits for them, and re-layouts: 9.2 us -> 6.38 us  [on_device(): got_part = swapped(sent_part, 'cluster', top_bit)[rev_slot]]
    dot_general x3 -> x4, matrix products: 20.3 us -> 21.5 us  [dot_trans(): lax.dot_general(operand, matrix, (((1,), (1,)), ((), ())), preferred_elem...]
  transfers between devices with their start and end apart: 3 -> 3, of which waited for: 3 -> 3; matrix products, arithmetic and copies ran while one was open for 4% -> 6% of each run, Pallas kernels for 0% -> 0%
where the time goes in v1:
time: 291 us
  waiting for transfers between devices  103 us (35%)
  blocking collectives  57.2 us (20%)
  matrix products  54.7 us (19%)
  local copies, waits for them, and re-layouts  52.5 us (18%)
  between operations  14.4 us (5%)
  other arithmetic  8.08 us (3%)
    all_gather x1, waiting for transfers between devices, on_device(): shard_piece = lax.all_gather(trip_blocks, 'narrow', axis=0, tiled=True)  69.8 us
    all_to_all x1, blocking collectives, side_by_side(): lax.all_to_all(both, axis, split_axis=split_dim, concat_axis=concat_dim,...  57.2 us
    ppermute x2, waiting for transfers between devices, swapped(): lax.ppermute(array, axis, [(i, i ^ 1 << bit) for i in range(lax.axis_size...  32.9 us
    dot_general x4, matrix products, dot_trans(): lax.dot_general(operand, matrix, (((1,), (1,)), ((), ())), preferred_elem...  21.5 us
    dot_general x1, local copies, waits for them, and re-layouts, on_device(): jnp.einsum('ksij,kif->ksjf', angle_mats, grad_blocks, preferred_element_t...  9 us
    reshape x1, local copies, waits for them, and re-layouts, on_device(): pair_terms.reshape(local_blocks, slot_count, block_edges * trip_width)  7.9 us
    dot_general x1, matrix products, on_device(): jnp.einsum('ksij,kif->ksjf', angle_mats, grad_blocks, preferred_element_t...  6.65 us
    gather x2, local copies, waits for them, and re-layouts, on_device(): got_part = swapped(sent_part, 'cluster', top_bit)[rev_slot]  6.38 us
  transfers between devices with their start and end apart: 3, of which 3 were waited for; matrix products, arithmetic and copies ran while one was open for 6% of the time, Pallas kernels for 0%

profile of v1, /device:TPU:1, one launch (start us, length us, event | category | flops | bytes accessed | tf_op | source)
XLA Modules:
  0.0 290.8 jit_solution(11666964646287774126)
XLA Ops:
  7.2 0.0 copy-start
  7.2 0.0 copy-start.11
  7.2 0.0 copy-start.6
  7.2 0.0 all-gather.2.cloned.1.call-start
  7.2 3.3 %multiply_convert_fusion.16 = (bf16[2048,64]{0,1:T(8,128)(2,1)S(1)}, f32[2048,64]{0,1:T(8,128)}) fusion(bf16[2048,512]{1,0:T(8,128)(2,1)} %param.10, bf16[512,64]{0,1:T(8,128)(2,1)} %param.12), kind=kOutput, calls=%fused_computation.45 | convolution fusion | flops 134873088 | bytes 2949120 | tf_op jit(solution)/shard_map/dot_general | solution.py:69
  10.6 0.3 copy.31
  10.9 0.0 copy-start.12
  10.9 0.0 copy-start.10
  10.9 1.2 reshape.110
  12.0 0.0 all-gather.2.cloned.1.call-update
  12.1 0.0 copy-done.11
  12.1 0.1 copy.30
  12.2 5.5 %reshape.112 = bf16[32,8,64,64]{3,2,1,0:T(8,128)(2,1)} reshape(bf16[32,8,4096]{2,1,0:T(8,128)(2,1)S(1)} %copy-done.6) | data formatting | bytes 4194304 | tf_op jit(solution)/shard_map/reshape | solution.py:68
  17.7 0.1 copy.40
  17.8 0.1 reshape.116
  17.9 0.1 copy.39
  18.0 0.1 reshape.115
  18.1 3.2 %sort.17 = (s32[256]{0:T(256)}, s32[256]{0:T(256)S(1)}) sort(s32[256]{0:T(256)S(1)} %reshape.115, s32[256]{0:T(256)S(1)} %iota.25), dimensions={0}, to_apply=%region_0.1 | sort | flops 2048 | bytes 4096 | tf_op jit(solution)/shard_map/jit(argsort)/sort | solution.py:122
  21.2 1.9 gather_fusion.3
  23.2 0.2 convert_element_type.182
  23.5 0.1 fusion.41
  23.5 0.1 reshape.120
  23.6 69.8 %all-gather.2.cloned.1.call-done = bf16[512,4096]{1,0:T(8,128)(2,1)} async-done(((bf16[32,4096]{1,0:T(8,128)(2,1)}), bf16[512,4096]{1,0:T(8,128)(2,1)}) %all-gather.2.cloned.1.call-update) | async-done | bytes 4194320 | tf_op jit(solution)/shard_map/all_gather | solution.py:72
  93.5 3.5 %convolution_convert_fusion = bf16[32,8,4096]{2,1,0:T(8,128)(2,1)S(1)} fusion(bf16[512,4096]{1,0:T(8,128)(2,1)} %all-gather.2.cloned.1.call-done, s32[32,8]{1,0:T(8,128)S(1)} %copy.30, pred[32,8]{1,0:T(8,128)(4,1)S(1)} %get-tuple-element.8), kind=kOutput, calls=%fused_computation.4 | convolution fusion | flops 1075052544 | bytes 6292736 | tf_op jit(solution)/shard_map/ksp,pf->ksf/dot_general | solution.py:75
  97.0 5.5 %reshape.111 = bf16[32,8,64,64]{3,2,1,0:T(8,128)(2,1)} reshape(bf16[32,8,4096]{2,1,0:T(8,128)(2,1)S(1)} %convolution_convert_fusion) | data formatting | bytes 4194304 | tf_op jit(solution)/shard_map/reshape | solution.py:76
  102.5 4.8 %fusion.10 = bf16[32,64,64]{1,2,0:T(8,128)(2,1)S(1)} fusion(bf16[32,8,64,64]{3,2,1,0:T(8,128)(2,1)} %reshape.111, bf16[32,8,64,64]{3,2,1,0:T(8,128)(2,1)} %reshape.112), kind=kOutput, calls=%fused_computation.37 | convolution fusion | flops 134348800 | bytes 4456448 | tf_op jit(solution)/shard_map/ksij,ksjf->kif/dot_general | solution.py:77
  107.3 0.3 copy.33
  107.6 0.5 convert_element_type.150
  108.1 0.3 copy.34
  108.4 0.7 collective-permute-start
  109.1 2.7 fusion.42
  111.8 22.8 %collective-permute-done = bf16[2048,64]{1,0:T(8,128)(2,1)S(1)} collective-permute-done((bf16[2048,64]{1,0:T(8,128)(2,1)S(1)}, bf16[2048,64]{1,0:T(8,128)(2,1)S(1)}, u32[]{:S(2)}, u32[]{:S(2)}) %collective-permute-start) | collective-permute-done | bytes 262176 | tf_op jit(solution)/shard_map/ppermute | solution.py:10
  134.5 6.2 %gather_fusion = bf16[2048,64]{1,0:T(8,128)(2,1)S(1)} fusion(bf16[2048,64]{1,0:T(8,128)(2,1)S(1)} %collective-permute-done, s32[2048]{0:T(1024)S(1)} %fusion.26), kind=kCustom, calls=%fused_computation | custom fusion | bytes 532480 | tf_op jit(solution)/shard_map/gather | solution.py:82
  140.7 0.7 fusion.43
  141.4 1.5 copy-done.4
  142.9 4.7 %fusion.3 = f32[2048,512]{1,0:T(8,128)S(1)} fusion(bf16[2048,512]{1,0:T(8,128)(2,1)} %param.10, bf16[1,512,512]{2,1,0:T(8,128)(2,1)S(1)} %copy-done.14, f32[2048,512]{1,0:T(8,128)S(1)} %copy-done.4, f32[2048,512]{1,0:T(8,128)S(1)} %fusion.43), kind=kOutput, calls=%fused_computation.29 | convolution fusion | flops 1092616192 | bytes 15204352 | tf_op jit(solution)/shard_map/dot_general | solution.py:88
  147.7 6.0 %multiply_convert_fusion.4 = (bf16[2048,512]{1,0:T(8,128)(2,1)}, f32[2048,512]{1,0:T(8,128)}) fusion(bf16[2048,512]{1,0:T(8,128)(2,1)S(1)} %copy-done.13, f32[2048,512]{1,0:T(8,128)S(1)} %copy-done.4, f32[2048,512]{1,0:T(8,128)S(1)} %fusion.43, bf16[1,512,512]{2,1,0:T(8,128)(2,1)S(1)} %copy-done, f32[2048,512]{1,0:T(8,128)S(1)} %fusion.3), kind=kOutput, calls=%fused_computation.15 | convolution fusion | flops 1104150528 | bytes 21495808 | tf_op jit(solution)/shard_map/dot_general | solution.py:90
  153.7 9.9 %fusion.1 = f32[2048,512]{1,0:T(8,128)} fusion(bf16[2048,512]{1,0:T(8,128)(2,1)} %param.11, f32[2048,512]{1,0:T(8,128)} %copy-done.15, f32[2048,512]{1,0:T(8,128)} %get-tuple-element.12, bf16[1,512,512]{2,1,0:T(8,128)(2,1)S(1)} %copy-done, bf16[1,512,512]{2,1,0:T(8,128)(2,1)S(1)} %copy-done.14), kind=kOutput, calls=%fused_computation.14 | convolution fusion | flops 2171600896 | bytes 15728640 | tf_op jit(solution)/shard_map/dot_general | solution.py:34
  163.5 5.4 %convolution_convert_fusion.1 = bf16[2048,64]{0,1:T(8,128)(2,1)S(1)} fusion(bf16[64,512]{1,0:T(8,128)(2,1)S(1)} %copy-done.8, f32[2048,512]{1,0:T(8,128)} %copy-done.3, f32[2048,512]{1,0:T(8,128)} %fusion.1), kind=kOutput, calls=%fused_computation.26 | convolution fusion | flops 147980288 | bytes 8716288 | tf_op jit(solution)/shard_map/dot_general | solution.py:34
  168.9 0.3 collective-permute-start.1
  169.3 0.2 copy-done.5
  169.5 1.9 fusion.8
  171.4 10.2 %collective-permute-done.1 = bf16[2048,64]{0,1:T(8,128)(2,1)S(1)} collective-permute-done((bf16[2048,64]{0,1:T(8,128)(2,1)S(1)}, bf16[2048,64]{0,1:T(8,128)(2,1)S(1)}, u32[]{:S(2)}, u32[]{:S(2)}) %collective-permute-start.1) | collective-permute-done | bytes 262176 | tf_op jit(solution)/shard_map/ppermute | solution.py:10
  181.6 0.3 copy.35
  181.9 6.2 %gather_fusion.1 = bf16[2048,64]{1,0:T(8,128)(2,1)S(1)} fusion(bf16[2048,64]{1,0:T(8,128)(2,1)S(1)} %copy.35, s32[2048]{0:T(1024)S(1)} %fusion.26), kind=kCustom, calls=%fused_computation.1 | custom fusion | bytes 532480 | tf_op jit(solution)/shard_map/gather | solution.py:108
  188.1 0.2 copy.36
  188.3 0.5 reshape.113
  188.8 6.6 %convolution_bitcast_fusion = f32[32,8,64,64]{2,3,1,0:T(8,128)} fusion(bf16[32,8,64,64]{3,2,1,0:T(8,128)(2,1)} %reshape.112, bf16[32,64,64,1]{1,0,2,3:T(8,128)(2,1)S(1)} %bitcast.52), kind=kOutput, calls=%fused_computation.25 | convolution fusion | flops 134217728 | bytes 6553600 | tf_op jit(solution)/shard_map/ksij,kif->ksjf/dot_general | solution.py:112
  195.5 9.0 %copy.38 = f32[32,8,64,64]{3,2,1,0:T(8,128)} copy(f32[32,8,64,64]{2,3,1,0:T(8,128)} %convolution_bitcast_fusion) | data formatting | bytes 8388608 | tf_op jit(solution)/shard_map/ksij,kif->ksjf/dot_general | solution.py:112
  204.5 7.9 %reshape.114 = f32[256,4096]{1,0:T(8,128)} reshape(f32[32,8,64,64]{3,2,1,0:T(8,128)} %copy.38) | data formatting | bytes 8388608 | tf_op jit(solution)/shard_map/reshape | solution.py:115
  212.4 2.6 broadcast_multiply_fusion
  215.0 3.2 %gather_fusion.2 = bf16[256,4096]{1,0:T(8,128)(2,1)} fusion(bf16[256,4096]{1,0:T(8,128)(2,1)S(1)} %broadcast_multiply_fusion, s32[1024]{0:T(1024)S(1)} %pad_clamp_fusion), kind=kCustom, calls=%fused_computation.2 | custom fusion | bytes 4195328 | tf_op jit(solution)/shard_map/gather | solution.py:123
  218.2 1.8 pad_maximum_fusion
  220.0 57.2 %all_to_all.5 = bf16[16,16,4097]{2,1,0:T(8,128)(2,1)S(1)} all-to-all(bf16[16,16,4097]{2,1,0:T(8,128)(2,1)S(1)} %pad_maximum_fusion), channel_id=1, replica_groups=mesh['cluster'=16,'narrow'=16] {'narrow'}, dimensions={0} | all-to-all | bytes 4195328 | tf_op jit(solution)/shard_map/all_to_all | solution.py:17
  277.2 0.3 convert_reduce_fusion
  277.5 0.1 convert_element_type.177
  277.6 0.3 slice.17
  277.9 0.0 copy-start.9
  277.9 0.4 fusion.22
  278.3 0.5 convolution_add_fusion
  278.9 0.0 copy-start.1
  278.9 0.4 reshape.119
  279.3 0.3 copy.42
  279.7 4.3 %add_convert_fusion = bf16[2048,512]{1,0:T(8,128)(2,1)} fusion(f32[2048,512]{1,0:T(8,128)} %fusion.1, bf16[512,64]{0,1:T(8,128)(2,1)S(1)} %copy-done.9, f32[2048,64]{0,1:T(8,128)S(1)} %copy.42, f32[2048,64]{0,1:T(8,128)S(1)} %copy-done.7), kind=kOutput, calls=%fused_computation.7 | convolution fusion | flops 138543104 | bytes 7405568 | tf_op jit(solution)/shard_map/dot_general | solution.py:34
  (29 shorter events, 0.1 us)
Async XLA Ops:
  7.2 140.5 %copy-start = (bf16[1,512,512]{2,1,0:T(8,128)(2,1)S(1)}, bf16[1,512,512]{2,1,0:T(8,128)(2,1)}, u32[]{:S(2)}) copy-start(bf16[1,512,512]{2,1,0:T(8,128)(2,1)} %param.15) | copy-start | bytes 1572868
  7.2 4.9 %copy-start.11 = (s32[32,8]{0,1:T(8,128)S(1)}, s32[32,8]{0,1:T(8,128)}, u32[]{:S(2)}) copy-start(s32[32,8]{0,1:T(8,128)} %param.18) | copy-start | bytes 3076
  7.2 5.0 %copy-start.6 = (bf16[32,8,4096]{2,1,0:T(8,128)(2,1)S(1)}, bf16[32,8,4096]{2,1,0:T(8,128)(2,1)}, u32[]{:S(2)}) copy-start(bf16[32,8,4096]{2,1,0:T(8,128)(2,1)} %param.16) | copy-start | bytes 6291460
  7.2 86.3 %all-gather.2.cloned.1.call-start = ((), (), s32[]{:S(2)}) async-start(), calls=%async_computation.1 | async-start | bytes 4456448 | tf_op jit(solution)/shard_map/all_gather | solution.py:72
  10.9 12.6 %copy-start.12 = (s32[32]{0:T(128)S(1)}, s32[32]{0:T(128)}, u32[]{:S(2)}) copy-start(s32[32]{0:T(128)} %param.19) | copy-start | bytes 388
  10.9 12.8 %copy-start.10 = (s32[2048]{0:T(1024)S(1)}, s32[2048]{0:T(1024)}, u32[]{:S(2)}) copy-start(s32[2048]{0:T(1024)} %param.17) | copy-start | bytes 24580
  102.5 6.6 %copy-start.8 = (bf16[64,512]{1,0:T(8,128)(2,1)S(1)}, bf16[64,512]{1,0:T(8,128)(2,1)}, u32[]{:S(2)}) copy-start(bf16[64,512]{1,0:T(8,128)(2,1)} %param.13) | copy-start | bytes 196612
  108.4 26.1 %collective-permute-start = (bf16[2048,64]{1,0:T(8,128)(2,1)S(1)}, bf16[2048,64]{1,0:T(8,128)(2,1)S(1)}, u32[]{:S(2)}, u32[]{:S(2)}) collective-permute-start(bf16[2048,64]{1,0:T(8,128)(2,1)S(1)} %copy.34), channel_id=1, source_target_pairs={{0,128},{16,144},{32,160},{48,176},{64,192},{80,208},{96,224},{112... | collective-permute-start | bytes 786440 | tf_op jit(solution)/shard_map/ppermute | solution.py:10
  111.8 29.6 %copy-start.14 = (bf16[1,512,512]{2,1,0:T(8,128)(2,1)S(1)}, bf16[1,512,512]{2,1,0:T(8,128)(2,1)}, u32[]{:S(2)}) copy-start(bf16[1,512,512]{2,1,0:T(8,128)(2,1)} %param.14) | copy-start | bytes 1572868
  140.7 2.2 copy-start.4
  142.9 4.7 %copy-start.3 = (f32[2048,512]{1,0:T(8,128)}, f32[2048,512]{1,0:T(8,128)S(1)}, u32[]{:S(2)}) copy-start(f32[2048,512]{1,0:T(8,128)S(1)} %fusion.43) | copy-start | bytes 12582916
  142.9 4.8 %copy-start.13 = (bf16[2048,512]{1,0:T(8,128)(2,1)S(1)}, bf16[2048,512]{1,0:T(8,128)(2,1)}, u32[]{:S(2)}) copy-start(bf16[2048,512]{1,0:T(8,128)(2,1)} %param.10) | copy-start | bytes 6291460
  147.7 6.0 %copy-start.15 = (f32[2048,512]{1,0:T(8,128)}, f32[2048,512]{1,0:T(8,128)S(1)}, u32[]{:S(2)}) copy-start(f32[2048,512]{1,0:T(8,128)S(1)} %fusion.3) | copy-start | bytes 12582916
  163.5 5.7 %copy-start.2 = (f32[2048,512]{1,0:T(8,128)S(1)}, f32[2048,512]{1,0:T(8,128)}, u32[]{:S(2)}) copy-start(f32[2048,512]{1,0:T(8,128)} %fusion.1) | copy-start | bytes 12582916
  163.5 5.9 %copy-start.5 = (f32[2048,512]{1,0:T(8,128)S(1)}, f32[2048,512]{1,0:T(8,128)}, u32[]{:S(2)}) copy-start(f32[2048,512]{1,0:T(8,128)} %fusion.42) | copy-start | bytes 12582916
  168.9 12.7 %collective-permute-start.1 = (bf16[2048,64]{0,1:T(8,128)(2,1)S(1)}, bf16[2048,64]{0,1:T(8,128)(2,1)S(1)}, u32[]{:S(2)}, u32[]{:S(2)}) collective-permute-start(bf16[2048,64]{0,1:T(8,128)(2,1)S(1)} %convolution_convert_fusion.1), channel_id=1, source_target_pairs={{0,128},{16,144},{32,160},{48,176},{64,192},{80,208},{96,224},{112... | collective-permute-start | bytes 786440 | tf_op jit(solution)/shard_map/ppermute | solution.py:10
  277.9 1.8 copy-start.7
  277.9 1.8 copy-start.9
  278.9 5.1 %copy-start.1 = (bf16[1,512,512]{2,1,0:T(8,128)(2,1)S(1)}, bf16[1,512,512]{2,1,0:T(8,128)(2,1)}, u32[]{:S(2)}) copy-start(bf16[1,512,512]{2,1,0:T(8,128)(2,1)} %param.15) | copy-start | bytes 1572868
Sparse Core Ops, SparseCore 0:
  12.2 81.2 all-gather.1

commit v2 on v0

v2 whole, which is shorter than its diff:
```python
import functools
import jax
import jax.numpy as jnp
from jax import lax
from jax.experimental import pallas as pl
from jax.experimental.pallas import tpu as pltpu
from jax.sharding import PartitionSpec as P

CH = 4


def place():
    me = lax.axis_index("narrow")
    core = lax.rem(me, 2)
    far = lax.rem(lax.div(me, 2), 2)
    row = lax.div(me, 4)
    return row, far, core


def slot_of(row, far, core):
    return (lax.rem(row + 4, 4) * 2 + far) * 2 + core


def greet(partners):
    barrier = pltpu.get_barrier_semaphore()
    for p in partners:
        pl.semaphore_signal(
            barrier, inc=1, device_id={"narrow": p}, device_id_type=pl.DeviceIdType.MESH
        )
    pl.semaphore_wait(barrier, len(partners))


def push(src, dst, send, recv, target):
    return pltpu.make_async_remote_copy(
        src_ref=src,
        dst_ref=dst,
        send_sem=send,
        recv_sem=recv,
        device_id={"narrow": target},
        device_id_type=pl.DeviceIdType.MESH,
    )


def gather_kernel(own, out, loc, ysend, yrecv, y2send, y2recv, zsend, zrecv, csend, crecv):
    row, far, core = place()
    up, dn = slot_of(row + 1, far, core), slot_of(row - 1, far, core)
    anti, sib = slot_of(row, 1 - far, core), slot_of(row, far, 1 - core)
    me = slot_of(row, far, core)
    rows = own.shape[0] // CH

    def part(ref, slot, q):
        return ref.at[slot, pl.ds(q * rows, rows)]

    greet((up, dn, anti, sib))
    keep = pltpu.make_async_copy(own, out.at[me], loc)
    keep.start()
    copies = []

    def go(c):
        c.start()
        copies.append(c)
        return c

    zc = [
        go(push(own.at[pl.ds(q * rows, rows)], part(out, me, q), zsend.at[q], zrecv.at[q], anti))
        for q in range(CH)
    ]
    order = {0: (0, 1, 2, 3), 1: (2, 3, 0, 1)}
    half = {0: (0, 1), 1: (2, 3)}
    nbr = (up, dn)
    yc = {}
    for i in range(CH):
        for d in (0, 1):
            q = order[d][i]
            yc[0, d, q] = go(
                push(
                    own.at[pl.ds(q * rows, rows)],
                    part(out, me, q),
                    ysend.at[0, d, q],
                    yrecv.at[0, d, q],
                    nbr[d],
                )
            )
    cc = [go(push(own, out.at[me], csend.at[0], crecv.at[0], sib))]

    def relay(z, d, q):
        yc[z, d, q].wait_recv()
        if q in half[d]:
            came = slot_of(row - 1 if d == 0 else row + 1, far if z == 0 else 1 - far, core)
            y2[z, q] = go(
                push(part(out, came, q), part(out, came, q), y2send.at[z, q], y2recv.at[z, q], nbr[d])
            )

    def to_sib(slot, i):
        cc.append(go(push(out.at[slot], out.at[slot], csend.at[i], crecv.at[i], sib)))

    y2 = {}
    for i in range(CH):
        for d in (0, 1):
            relay(0, d, order[d][i])
    to_sib(dn, 1)
    to_sib(up, 2)
    for q in range(CH):
        zc[q].wait_recv()
        for d in (0, 1):
            yc[1, d, q] = go(
                push(part(out, anti, q), part(out, anti, q), ysend.at[1, d, q], yrecv.at[1, d, q], nbr[d])
            )
    to_sib(anti, 3)
    for q in range(CH):
        y2[0, q].wait_recv()
    to_sib(slot_of(row + 2, far, core), 4)
    for i in range(CH):
        for d in (0, 1):
            relay(1, d, order[d][i])
    to_sib(slot_of(row - 1, 1 - far, core), 5)
    to_sib(slot_of(row + 1, 1 - far, core), 6)
    for q in range(CH):
        y2[1, q].wait_recv()
    to_sib(slot_of(row + 2, 1 - far, core), 7)
    for c in cc:
        c.wait_recv()
    for c in copies:
        c.wait_send()
    keep.wait()


def all_gather(own):
    dma = pltpu.SemaphoreType.DMA
    return pl.pallas_call(
        gather_kernel,
        name="gather_narrow",
        out_shape=jax.ShapeDtypeStruct((16, *own.shape), own.dtype),
        in_specs=[pl.BlockSpec(memory_space=pl.ANY)],
        out_specs=pl.BlockSpec(memory_space=pl.ANY),
        scratch_shapes=[
            dma,
            dma((2, 2, CH)),
            dma((2, 2, CH)),
            dma((2, CH)),
            dma((2, CH)),
            dma((CH,)),
            dma((CH,)),
            dma((8,)),
            dma((8,)),
        ],
        compiler_params=pltpu.CompilerParams(collective_id=0, has_side_effects=True),
    )(own)


def scatter_kernel(parts, out, near_buf, y2buf, ybuf, zbuf, stage, psend, precv, y2send, y2recv, ysend, yrecv, zsend, zrecv):
    row, far, core = place()
    up, dn = slot_of(row + 1, far, core), slot_of(row - 1, far, core)
    anti, sib = slot_of(row, 1 - far, core), slot_of(row, far, 1 - core)
    nbr = (up, dn)
    rows = out.shape[0] // CH
    half = {0: (0, 1), 1: (2, 3)}
    greet((up, dn, anti, sib))
    copies = []

    def go(c):
        c.start()
        copies.append(c)
        return c

    def far_of(z):
        return 1 - far if z == 0 else far

    hops = (2, 1, 3, 0)
    sc = {}
    for z in (0, 1):
        for o in hops:
            dest = slot_of(row + o, far_of(z), 1 - core)
            sc[z, o] = go(
                push(parts.at[dest], near_buf.at[z, o], psend.at[z, o], precv.at[z, o], sib)
            )

    def chip_sum(z, o, q):
        sl = pl.ds(q * rows, rows)
        mine = parts[slot_of(row + o, far_of(z), core), sl].astype(jnp.float32)
        return mine + near_buf[z, o, sl].astype(jnp.float32)

    y2, yc, zc = {}, {}, {}

    def send_y2(z):
        sc[z, 2].wait_recv()
        for d in (0, 1):
            for q in half[d]:
                sl = pl.ds(q * rows, rows)
                stage[z, 2, sl] = chip_sum(z, 2, q).astype(jnp.bfloat16)
                y2[z, q] = go(
                    push(stage.at[z, 2, sl], y2buf.at[z, sl], y2send.at[z, q], y2recv.at[z, q], nbr[d])
                )

    def send_y(z):
        for d, o in ((0, 1), (1, 3)):
            sc[z, o].wait_recv()
        for d, o in ((0, 1), (1, 3)):
            for q in half[1 - d]:
                sl = pl.ds(q * rows, rows)
                stage[z, o, sl] = chip_sum(z, o, q).astype(jnp.bfloat16)
                yc[z, d, q] = go(
                    push(stage.at[z, o, sl], ybuf.at[z, d, sl], ysend.at[z, d, q], yrecv.at[z, d, q], nbr[d])
                )
        for i in (0, 1):
            for d, o in ((0, 1), (1, 3)):
                q = half[d][i]
                sl = pl.ds(q * rows, rows)
                y2[z, q].wait_recv()
                stage[z, o, sl] = (
                    chip_sum(z, o, q) + y2buf[z, sl].astype(jnp.float32)
                ).astype(jnp.bfloat16)
                yc[z, d, q] = go(
                    push(stage.at[z, o, sl], ybuf.at[z, d, sl], ysend.at[z, d, q], yrecv.at[z, d, q], nbr[d])
                )

    def final(z, q):
        sl = pl.ds(q * rows, rows)
        yc[z, 0, q].wait_recv()
        yc[z, 1, q].wait_recv()
        return (
            chip_sum(z, 0, q)
            + ybuf[z, 0, sl].astype(jnp.float32)
            + ybuf[z, 1, sl].astype(jnp.float32)
        )

    send_y2(0)
    send_y(0)
    send_y2(1)
    sc[0, 0].wait_recv()
    for q in (2, 0, 3, 1):
        sl = pl.ds(q * rows, rows)
        stage[0, 0, sl] = final(0, q).astype(jnp.bfloat16)
        zc[q] = go(push(stage.at[0, 0, sl], zbuf.at[sl], zsend.at[q], zrecv.at[q], anti))
    send_y(1)
    sc[1, 0].wait_recv()
    for q in (2, 0, 3, 1):
        sl = pl.ds(q * rows, rows)
        out[sl] = final(1, q)
    for q in (2, 0, 3, 1):
        sl = pl.ds(q * rows, rows)
        zc[q].wait_recv()
        out[sl] = out[sl] + zbuf[sl].astype(jnp.float32)
    for c in copies:
        c.wait_send()


def reduce_scatter(parts):
    dma = pltpu.SemaphoreType.DMA
    n, r, l = parts.shape
    vm = pltpu.VMEM
    return pl.pallas_call(
        scatter_kernel,
        name="scatter_narrow",
        out_shape=jax.ShapeDtypeStruct((r, l), jnp.float32),
        in_specs=[pl.BlockSpec(memory_space=pltpu.VMEM)],
        out_specs=pl.BlockSpec(memory_space=pltpu.VMEM),
        scratch_shapes=[
            vm((2, 4, r, l), jnp.bfloat16),
            vm((2, r, l), jnp.bfloat16),
            vm((2, 2, r, l), jnp.bfloat16),
            vm((r, l), jnp.bfloat16),
            vm((2, 4, r, l), jnp.bfloat16),
            dma((2, 4)),
            dma((2, 4)),
            dma((2, CH)),
            dma((2, CH)),
            dma((2, 2, CH)),
            dma((2, 2, CH)),
            dma((CH,)),
            dma((CH,)),
        ],
        compiler_params=pltpu.CompilerParams(collective_id=1, has_side_effects=True),
    )(parts)


ROOT_HALF = 0.7071067811865476
TILES = 8


def sigmoid(v):
    return 0.5 + 0.5 * jnp.tanh(0.5 * v)


def silu_both(v):
    s = sigmoid(v)
    f = v * s
    return f, s + f * (1.0 - s)


def low_lanes(shape):
    return lax.broadcasted_iota(jnp.int32, shape, len(shape) - 1) < 64


def swap_halves(v):
    return pltpu.roll(v, 64, 1)


def dot(a, b):
    return jnp.dot(a, b, preferred_element_type=jnp.float32)


def dot_rows(a, b):
    return lax.dot_general(a, b, (((1,), (1,)), ((), ())), preferred_element_type=jnp.float32)


def dot_cols(a, b):
    return lax.dot_general(a, b, (((0,), (0,)), ((), ())), preferred_element_type=jnp.float32)


def paired(v):
    n = v.shape[0] // 64
    v = v.reshape(n, 2, 32, 128)
    return jnp.where(low_lanes((n, 32, 128)), v[:, 0], v[:, 1]).reshape(n * 32, 128)


def spread(t):
    n = t.shape[0] // 32
    t = t.reshape(n, 32, 128)
    low = low_lanes(t.shape)
    zero = jnp.zeros_like(t)
    both = jnp.concatenate([jnp.where(low, t, zero), jnp.where(low, zero, t)], axis=1)
    return both.reshape(n * 64, 128)


def pick_rows(rev, table):
    edge = lax.rem(rev, 2048)
    block, rest = lax.div(edge, 64), lax.rem(edge, 64)
    row = block * 32 + lax.rem(rest, 32)
    upper = rest >= 32
    hot = lax.broadcasted_iota(jnp.int32, (rev.shape[0], table.shape[0]), 1) == row
    hot = jnp.where(hot, 1.0, 0.0).astype(jnp.bfloat16)
    got = dot(hot, table)
    return jnp.where(low_lanes(got.shape) != upper, got, 0.0)


def prep_kernel(x, wd2, ang, trip, pre, amat, tmp):
    pair = paired(dot(x[...], wd2[...]))
    pre[...] = pair
    trip[...] = (pair * sigmoid(pair)).astype(jnp.bfloat16)
    low = low_lanes((64, 128))

    def one(k, carry):
        a = ang[k].astype(jnp.float32)
        for r in range(32):
            t = a[:, 128 * r : 128 * r + 128]
            tmp[16 * r : 16 * r + 8] = t
            tmp[16 * r + 8 : 16 * r + 16] = swap_halves(t)
        for s in range(0, 8, 2):
            first = tmp[pl.ds(s, 64, stride=8), :]
            second = tmp[pl.ds(s + 1, 64, stride=8), :]
            both = jnp.where(low, first, swap_halves(second)).astype(jnp.bfloat16)
            amat[pl.ds(pl.multiple_of(k * 64, 64), 64), s * 64 : s * 64 + 128] = both
        return carry

    lax.fori_loop(0, ang.shape[0], one, 0)


def prep(x, wd2, ang):
    n = x.shape[0]
    t = n // TILES
    return pl.pallas_call(
        prep_kernel,
        name="prep",
        grid=(TILES,),
        in_specs=[
            pl.BlockSpec((t, x.shape[1]), lambda i: (i, 0)),
            pl.BlockSpec(wd2.shape, lambda i: (0, 0)),
            pl.BlockSpec((t // 64, 8, 4096), lambda i: (i, 0, 0)),
        ],
        out_specs=[
            pl.BlockSpec((t // 2, 128), lambda i: (i, 0)),
            pl.BlockSpec((t // 2, 128), lambda i: (i, 0)),
            pl.BlockSpec((t, 512), lambda i: (i, 0)),
        ],
        out_shape=[
            jax.ShapeDtypeStruct((n // 2, 128), jnp.bfloat16),
            jax.ShapeDtypeStruct((n // 2, 128), jnp.float32),
            jax.ShapeDtypeStruct((n, 512), jnp.bfloat16),
        ],
        scratch_shapes=[pltpu.VMEM((512, 128), jnp.float32)],
    )(x, wd2, ang)


def blocks_kernel(src, cnt, trips, amat, out, rhs):
    i = pl.program_id(0)
    nk = amat.shape[0] // 64
    for k in range(nk):
        g = i * nk + k
        live = cnt[g]
        for s in range(8):
            b = lax.rem(src[g * 8 + s], 512)
            q = trips[pl.ds(pl.multiple_of(b * 32, 32), 32), :]
            q = jnp.where(s < live, q, jnp.zeros_like(q))
            rhs[k, s * 64 : s * 64 + 32] = q
            rhs[k, s * 64 + 32 : s * 64 + 64] = swap_halves(q)
        o = dot(amat[k * 64 : k * 64 + 64], rhs[k])
        pair = jnp.where(low_lanes((32, 128)), o[:32], swap_halves(o[32:]))
        out[k * 32 : k * 32 + 32] = pair.astype(jnp.bfloat16)


def blocks(src, cnt, trips, amat):
    n = amat.shape[0]
    t = n // TILES
    return pl.pallas_call(
        blocks_kernel,
        name="blocks",
        grid_spec=pltpu.PrefetchScalarGridSpec(
            num_scalar_prefetch=2,
            grid=(TILES,),
            in_specs=[
                pl.BlockSpec(trips.shape, lambda i, *_: (0, 0), pipeline_mode=pl.Buffered(1)),
                pl.BlockSpec((t, 512), lambda i, *_: (i, 0)),
            ],
            out_specs=pl.BlockSpec((t // 2, 128), lambda i, *_: (i, 0)),
            scratch_shapes=[pltpu.VMEM((t // 64, 512, 128), jnp.bfloat16)],
        ),
        out_shape=jax.ShapeDtypeStruct((n // 2, 128), jnp.bfloat16),
    )(src, cnt, trips, amat)


def layer_kernel(x, cot, own, theirs, rev, ww, wi, wo, out, gmsg, hsend, gown):
    c = ROOT_HALF
    w2 = ww[...]
    up, dup = silu_both(dot(spread(own[...]), w2))
    picked = pick_rows(rev[...], theirs[...]).astype(jnp.bfloat16)
    pup, dpup = silu_both(dot(picked, w2))
    up = up.astype(jnp.bfloat16).astype(jnp.float32)
    pup = pup.astype(jnp.bfloat16).astype(jnp.float32)
    hidden = (x[...].astype(jnp.float32) + (up + pup) * c) * c
    act, dact = silu_both(dot(hidden.astype(jnp.bfloat16), wi[...]))
    res, dres = silu_both(dot(act.astype(jnp.bfloat16), wo[...]))
    out[...] = ((hidden + res) * c).astype(jnp.bfloat16)
    scaled = cot[...].astype(jnp.float32) * c
    grad_out = (scaled * dres).astype(jnp.bfloat16)
    grad_in = (dot_rows(grad_out, wo[...]) * dact).astype(jnp.bfloat16)
    grad_msg = (scaled + dot_rows(grad_in, wi[...])) * c
    gmsg[...] = grad_msg
    rounded = grad_msg.astype(jnp.bfloat16).astype(jnp.float32)
    hsend[...] = paired(dot_rows((rounded * (c * dpup)).astype(jnp.bfloat16), w2)).astype(jnp.bfloat16)
    gown[...] = dot_rows((grad_msg * (c * dup)).astype(jnp.bfloat16), w2)


def layer(x, cot, own, theirs, rev, ww, wi, wo):
    n, d = x.shape
    t = n // TILES
    wide = pl.BlockSpec((t, d), lambda i: (i, 0))

    def whole(a):
        return pl.BlockSpec(a.shape, lambda i: (0, 0))

    return pl.pallas_call(
        layer_kernel,
        name="layer",
        grid=(TILES,),
        in_specs=[
            wide,
            wide,
            pl.BlockSpec((t // 2, 128), lambda i: (i, 0)),
            whole(theirs),
            pl.BlockSpec((t, 1), lambda i: (i, 0)),
            whole(ww),
            whole(wi),
            whole(wo),
        ],
        out_specs=[
            wide,
            wide,
            pl.BlockSpec((t // 2, 128), lambda i: (i, 0)),
            pl.BlockSpec((t, 128), lambda i: (i, 0)),
        ],
        out_shape=[
            jax.ShapeDtypeStruct((n, d), jnp.bfloat16),
            jax.ShapeDtypeStruct((n, d), jnp.float32),
            jax.ShapeDtypeStruct((n // 2, 128), jnp.bfloat16),
            jax.ShapeDtypeStruct((n, 128), jnp.float32),
        ],
    )(x, cot, own, theirs, rev, ww, wi, wo)


def terms_kernel(src, cnt, got, rev, gown, amat, out, acc):
    i = pl.program_id(0)
    nk = amat.shape[0] // 64

    @pl.when(i == 0)
    def _():
        acc[...] = jnp.zeros_like(acc)

    theirs = pick_rows(rev[...], got[...])
    grad = (gown[...] + theirs + swap_halves(theirs)).astype(jnp.bfloat16)
    for k in range(nk):
        g = i * nk + k
        o = dot_cols(amat[k * 64 : k * 64 + 64], grad[k * 64 : k * 64 + 64])
        pair = paired(o)
        live = cnt[g]
        for s in range(8):
            b = lax.rem(src[g * 8 + s], 512)

            @pl.when(s < live)
            def _(b=b, s=s, pair=pair):
                acc[pl.ds(pl.multiple_of(b * 32, 32), 32), :] += pair[s * 32 : s * 32 + 32]

    @pl.when(i == TILES - 1)
    def _():
        out[...] = acc[...].astype(jnp.bfloat16)


def terms(src, cnt, got, rev, gown, amat):
    n = amat.shape[0]
    t = n // TILES
    return pl.pallas_call(
        terms_kernel,
        name="terms",
        grid_spec=pltpu.PrefetchScalarGridSpec(
            num_scalar_prefetch=2,
            grid=(TILES,),
            in_specs=[
                pl.BlockSpec(got.shape, lambda i, *_: (0, 0)),
                pl.BlockSpec((t, 1), lambda i, *_: (i, 0)),
                pl.BlockSpec((t, 128), lambda i, *_: (i, 0)),
                pl.BlockSpec((t, 512), lambda i, *_: (i, 0)),
            ],
            out_specs=pl.BlockSpec((16384, 128), lambda i, *_: (0, 0), pipeline_mode=pl.Buffered(1)),
            scratch_shapes=[pltpu.VMEM((16384, 128), jnp.float32)],
        ),
        out_shape=jax.ShapeDtypeStruct((16384, 128), jnp.bfloat16),
    )(src, cnt, got, rev, gown, amat)


def last_kernel(gmsg, total, pre, wd2, out):
    grad = (total[...] * silu_both(pre[...])[1]).astype(jnp.bfloat16)
    out[...] = (gmsg[...] + dot_rows(spread(grad), wd2[...])).astype(jnp.bfloat16)


def last(gmsg, total, pre, wd2):
    n, d = gmsg.shape
    t = n // TILES
    wide = pl.BlockSpec((t, d), lambda i: (i, 0))
    slim = pl.BlockSpec((t // 2, 128), lambda i: (i, 0))
    return pl.pallas_call(
        last_kernel,
        name="last",
        grid=(TILES,),
        in_specs=[wide, slim, slim, pl.BlockSpec(wd2.shape, lambda i: (0, 0))],
        out_specs=wide,
        out_shape=jax.ShapeDtypeStruct((n, d), jnp.bfloat16),
    )(gmsg, total, pre, wd2)


def mirrored(v):
    size = lax.axis_size("cluster")
    return lax.ppermute(v, "cluster", [(i, i ^ (size // 2)) for i in range(size)])


def on_device(x, cot, down, up, inner, outer, ang, reverse, sources, counts):
    wd2 = jnp.concatenate([down, down], axis=1)
    ww = jnp.concatenate([up, up], axis=0)
    src = sources.reshape(-1)
    rev = reverse.reshape(-1, 1)
    trip, pre, amat = prep(x, wd2, ang)
    trips = all_gather(trip).reshape(-1, 128)
    own = blocks(src, counts, trips, amat)
    theirs = mirrored(own)
    out, gmsg, hsend, gown = layer(x, cot, own, theirs, rev, ww, inner[0], outer[0])
    got = mirrored(hsend)
    parts = terms(src, counts, got, rev, gown, amat)
    total = reduce_scatter(parts.reshape(16, -1, 128))
    return out, last(gmsg, total, pre, wd2)


def solution(mesh):
    rows = P(("cluster", "narrow"))
    specs = (rows, rows, P(), P(), P(), P(), rows, rows, rows, rows)
    return jax.shard_map(
        on_device, mesh=mesh, in_specs=specs, out_specs=(rows, rows), check_vma=False
    )
```

time: 370 us -> 162 us (0.44)
  waiting for transfers between devices: 184 us -> 24.5 us
  Pallas kernels: 0 us -> 126 us
  blocking collectives: 57.4 us -> 0 us
  matrix products: 52 us -> 0 us
  local copies, waits for them, and re-layouts: 53.4 us -> 5.2 us
  between operations: 14.3 us -> 0.69 us
  other arithmetic: 8.01 us -> 1.42 us
    pallas_call x0 -> x7, Pallas kernels: none -> 126 us  [the longest x1 32.5 us: all_gather(): pl.pallas_call(gather_kernel, name='gather_narrow', out_shape=jax.ShapeDt...]
    ppermute x2, waiting for transfers between devices: 108 us -> 24.5 us  [mirrored(): return lax.ppermute(v, 'cluster', [(i, i ^ size // 2) for i in range(size)])]
    all_gather x1 -> x0, waiting for transfers between devices: 75.6 us -> none  [on_device(): shard_piece = lax.all_gather(trip_blocks, 'narrow', axis=0, tiled=True)]
    all_to_all x1 -> x0, blocking collectives: 57.4 us -> none  [side_by_side(): lax.all_to_all(both, axis, split_axis=split_dim, concat_axis=concat_dim,...]
    dot_general x13 -> x0, matrix products: 52 us -> none  [the longest x3 20.3 us: dot_trans(): lax.dot_general(operand, matrix, (((1,), (1,)), ((), ())), preferred_elem...]
    gather x4 -> x0, local copies, waits for them, and re-layouts: 20.5 us -> none  [the longest x1 9.2 us: on_device(): partner_grad = swapped(grad_msg_round, 'cluster', top_bit)[rev_slot]]
    reshape x9 -> x2, local copies, waits for them, and re-layouts: 21.6 us -> 2.05 us  [the longest x1 1.42 us: on_device(): rev = reverse.reshape(-1, 1)]
    dot_general x1 -> x0, local copies, waits for them, and re-layouts: 8.99 us -> none  [on_device(): jnp.einsum('ksij,kif->ksjf', angle_mats, grad_blocks, preferred_element_t...]
  transfers between devices with their start and end apart: 3 -> 2, of which waited for: 3 -> 2; matrix products, arithmetic and copies ran while one was open for 4% -> 1% of each run, Pallas kernels for 0% -> 0%
where the time goes in v2:
time: 162 us; the launch traced here: 161 us
  Pallas kernels  126 us (78%)
  waiting for transfers between devices  24.5 us (15%)
  local copies, waits for them, and re-layouts  5.2 us (3%)
  starting transfers between devices  2.79 us (2%)
    pallas_call x1, Pallas kernels, all_gather(): pl.pallas_call(gather_kernel, name='gather_narrow', out_shape=jax.ShapeDt...  32.5 us
    pallas_call x1, Pallas kernels, reduce_scatter(): pl.pallas_call(scatter_kernel, name='scatter_narrow', out_shape=jax.Shape...  31.3 us
    ppermute x2, waiting for transfers between devices, mirrored(): return lax.ppermute(v, 'cluster', [(i, i ^ size // 2) for i in range(size)])  24.5 us
    pallas_call x1, Pallas kernels, layer(): pl.pallas_call(layer_kernel, name='layer', grid=(TILES,), in_specs=[wide,...  18.8 us
    pallas_call x1, Pallas kernels, terms(): pl.pallas_call(terms_kernel, name='terms', grid_spec=pltpu.PrefetchScalar...  17 us
    pallas_call x1, Pallas kernels, prep(): pl.pallas_call(prep_kernel, name='prep', grid=(TILES,), in_specs=[pl.Bloc...  10.2 us
    pallas_call x1, Pallas kernels, blocks(): pl.pallas_call(blocks_kernel, name='blocks', grid_spec=pltpu.PrefetchScal...  9.26 us
    pallas_call x1, Pallas kernels, last(): pl.pallas_call(last_kernel, name='last', grid=(TILES,), in_specs=[wide, s...  7.08 us
  transfers between devices with their start and end apart: 2, of which 2 were waited for; matrix products, arithmetic and copies ran while one was open for 1% of the time, Pallas kernels for 0%

profile of v2, /device:TPU:1, one launch (start us, length us, event | category | flops | bytes accessed | tf_op | source)
XLA Modules:
  0.0 160.7 jit_solution(11715108790464033422)
XLA Ops:
  0.6 0.8 copy.14
  1.4 0.6 reshape.16.src
  2.0 1.0 copy.15
  3.0 0.8 pad_maximum_fusion.wd2
  3.7 10.2 %prep.1 = (bf16[1024,128]{1,0:T(8,128)(2,1)}, f32[1024,128]{1,0:T(8,128)}, bf16[2048,512]{1,0:T(8,128)(2,1)}) custom-call(bf16[2048,512]{1,0:T(8,128)(2,1)} %x.3, bf16[512,128]{1,0:T(8,128)(2,1)} %pad_maximum_fusion.wd2, bf16[32,8,4096]{2,1,0:T(8,128)(2,1)} %ang.1), custom_call_target="tpu_custom_call" | custom-call | tf_op jit(solution)/shard_map/prep/pallas_call | solution.py:362
  14.0 32.5 %gather_narrow.1 = bf16[16,1024,128]{2,1,0:T(8,128)(2,1)} custom-call(bf16[1024,128]{1,0:T(8,128)(2,1)} %get-tuple-element.9.own), custom_call_target="tpu_custom_call" | custom-call | tf_op jit(solution)/shard_map/gather_narrow/pallas_call | solution.py:130
  46.5 0.0 copy-start.3
  46.5 0.0 copy-start.2
  46.5 9.3 %blocks.1.own = bf16[1024,128]{1,0:T(8,128)(2,1)} custom-call(s32[256]{0:T(256)} %reshape.16.src, s32[32]{0:T(128)} %cnt.3, bf16[16384,128]{1,0:T(8,128)(2,1)} %bitcast.6, bf16[2048,512]{1,0:T(8,128)(2,1)} %get-tuple-element.10.amat), custom_call_target="tpu_custom_call" | custom-call | tf_op jit(solution)/shard_map/blocks/pallas_call | solution.py:405
  55.8 2.7 %collective-permute-start = (bf16[1024,128]{1,0:T(8,128)(2,1)}, bf16[1024,128]{1,0:T(8,128)(2,1)S(1)}, u32[]{:S(2)}, u32[]{:S(2)}) collective-permute-start(bf16[1024,128]{1,0:T(8,128)(2,1)} %blocks.1.own), channel_id=1, source_target_pairs={{0,128},{16,144},{32,160},{48,176},{64,192},{80,208},{96,224},{112... | collective-permute-start | bytes 786440 | tf_op jit(solution)/shard_map/ppermute | solution.py:552
  58.4 0.0 copy-done.3
  58.4 1.4 copy.17.rev
  59.9 0.0 copy-done.2
  59.9 0.7 pad_maximum_fusion.1.ww
  60.5 10.3 %collective-permute-done.theirs = bf16[1024,128]{1,0:T(8,128)(2,1)S(1)} collective-permute-done((bf16[1024,128]{1,0:T(8,128)(2,1)}, bf16[1024,128]{1,0:T(8,128)(2,1)S(1)}, u32[]{:S(2)}, u32[]{:S(2)}) %collective-permute-start) | collective-permute-done | bytes 262176 | tf_op jit(solution)/shard_map/ppermute | solution.py:552
  70.9 0.0 copy-start.1
  70.9 0.7 copy-done.1
  71.6 18.8 %layer.1 = (bf16[2048,512]{1,0:T(8,128)(2,1)}, f32[2048,512]{1,0:T(8,128)}, bf16[1024,128]{1,0:T(8,128)(2,1)}, f32[2048,128]{1,0:T(8,128)}) custom-call(bf16[2048,512]{1,0:T(8,128)(2,1)} %x.3, bf16[2048,512]{1,0:T(8,128)(2,1)} %cot.1, bf16[1024,128]{1,0:T(8,128)(2,1)} %blocks.1.own, bf16[1024,128]{1,0:T(8,128)(2,1)} %copy-done.1, s32[2048,1]{1,0:T(8,128)} %copy.17.rev, ...), custom_call_target="tpu_custom_call" | custom-call | tf_op jit(solution)/shard_map/layer/pallas_call | solution.py:452
  90.4 0.1 collective-permute-start.1
  90.5 14.2 %collective-permute-done.1.got = bf16[1024,128]{1,0:T(8,128)(2,1)S(1)} collective-permute-done((bf16[1024,128]{1,0:T(8,128)(2,1)}, bf16[1024,128]{1,0:T(8,128)(2,1)S(1)}, u32[]{:S(2)}, u32[]{:S(2)}) %collective-permute-start.1) | collective-permute-done | bytes 262176 | tf_op jit(solution)/shard_map/ppermute | solution.py:552
  104.7 0.0 copy-start
  104.7 0.7 copy-done
  105.4 17.0 %terms.1 = bf16[16384,128]{1,0:T(8,128)(2,1)} custom-call(s32[256]{0:T(256)} %reshape.16.src, s32[32]{0:T(128)} %cnt.3, bf16[1024,128]{1,0:T(8,128)(2,1)} %copy-done, s32[2048,1]{1,0:T(8,128)} %copy.17.rev, f32[2048,128]{1,0:T(8,128)} %get-tuple-element.14.gown, bf16[2048,512]{1,0:T(8,128)(2,1)} %get-tuple-element.10.amat), custom_call_target="tpu_custom_call" | custom-call | tf_op jit(solution)/shard_map/terms/pallas_call | solution.py:511
  122.3 31.3 %scatter_narrow.1.total = f32[1024,128]{1,0:T(8,128)} custom-call(bf16[16,1024,128]{2,1,0:T(8,128)(2,1)} %bitcast.5), custom_call_target="tpu_custom_call" | custom-call | tf_op jit(solution)/shard_map/scatter_narrow/pallas_call | solution.py:252
  153.6 7.1 %last.1 = bf16[2048,512]{1,0:T(8,128)(2,1)} custom-call(f32[2048,512]{1,0:T(8,128)} %get-tuple-element.12.gmsg, f32[1024,128]{1,0:T(8,128)} %scatter_narrow.1.total, f32[1024,128]{1,0:T(8,128)} %get-tuple-element.15.pre, bf16[512,128]{1,0:T(8,128)(2,1)} %pad_maximum_fusion.wd2), custom_call_target="tpu_custom_call" | custom-call | tf_op jit(solution)/shard_map/last/pallas_call | solution.py:540
Async XLA Ops:
  46.5 12.0 %copy-start.3 = (s32[2048]{0:T(1024)S(1)}, s32[2048]{0:T(1024)}, u32[]{:S(2)}) copy-start(s32[2048]{0:T(1024)} %param.17) | copy-start | bytes 24580
  46.5 13.4 %copy-start.2 = (bf16[64,512]{1,0:T(8,128)(2,1)S(1)}, bf16[64,512]{1,0:T(8,128)(2,1)}, u32[]{:S(2)}) copy-start(bf16[64,512]{1,0:T(8,128)(2,1)} %param.13) | copy-start | bytes 196612
  55.8 15.1 %collective-permute-start = (bf16[1024,128]{1,0:T(8,128)(2,1)}, bf16[1024,128]{1,0:T(8,128)(2,1)S(1)}, u32[]{:S(2)}, u32[]{:S(2)}) collective-permute-start(bf16[1024,128]{1,0:T(8,128)(2,1)} %blocks.1.own), channel_id=1, source_target_pairs={{0,128},{16,144},{32,160},{48,176},{64,192},{80,208},{96,224},{112... | collective-permute-start | bytes 786440 | tf_op jit(solution)/shard_map/ppermute | solution.py:552
  70.9 0.7 copy-start.1
  90.4 14.3 %collective-permute-start.1 = (bf16[1024,128]{1,0:T(8,128)(2,1)}, bf16[1024,128]{1,0:T(8,128)(2,1)S(1)}, u32[]{:S(2)}, u32[]{:S(2)}) collective-permute-start(bf16[1024,128]{1,0:T(8,128)(2,1)} %get-tuple-element.13), channel_id=1, source_target_pairs={{0,128},{16,144},{32,160},{48,176},{64,192},{80,208},{96,224},{112... | collective-permute-start | bytes 786440 | tf_op jit(solution)/shard_map/ppermute | solution.py:552
  104.7 0.7 copy-start

commit v3 on v0

v3 whole, which is shorter than its diff:
```python
import functools
import jax
import jax.numpy as jnp
from jax import lax
from jax.experimental import pallas as pl
from jax.experimental.pallas import tpu as pltpu
from jax.sharding import PartitionSpec as P

CH = 4


def place():
    me = lax.axis_index("narrow")
    core = lax.rem(me, 2)
    far = lax.rem(lax.div(me, 2), 2)
    row = lax.div(me, 4)
    return row, far, core


def slot_of(row, far, core):
    return (lax.rem(row + 4, 4) * 2 + far) * 2 + core


ROOT_HALF = 0.7071067811865476
TILES = 8


def sigmoid(v):
    return 0.5 + 0.5 * jnp.tanh(0.5 * v)


def silu_both(v):
    s = sigmoid(v)
    f = v * s
    return f, s + f * (1.0 - s)


def low_lanes(shape):
    return lax.broadcasted_iota(jnp.int32, shape, len(shape) - 1) < 64


def swap_halves(v):
    return pltpu.roll(v, 64, 1)


def dot(a, b):
    return jnp.dot(a, b, preferred_element_type=jnp.float32)


def dot_rows(a, b):
    return lax.dot_general(a, b, (((1,), (1,)), ((), ())), preferred_element_type=jnp.float32)


def dot_cols(a, b):
    return lax.dot_general(a, b, (((0,), (0,)), ((), ())), preferred_element_type=jnp.float32)


def paired(v):
    n = v.shape[0] // 64
    v = v.reshape(n, 2, 32, 128)
    return jnp.where(low_lanes((n, 32, 128)), v[:, 0], v[:, 1]).reshape(n * 32, 128)


def spread(t):
    n = t.shape[0] // 32
    t = t.reshape(n, 32, 128)
    low = low_lanes(t.shape)
    zero = jnp.zeros_like(t)
    both = jnp.concatenate([jnp.where(low, t, zero), jnp.where(low, zero, t)], axis=1)
    return both.reshape(n * 64, 128)


def pick_rows(rev, table):
    edge = lax.rem(rev, 2048)
    block, rest = lax.div(edge, 64), lax.rem(edge, 64)
    row = block * 32 + lax.rem(rest, 32)
    upper = rest >= 32
    hot = lax.broadcasted_iota(jnp.int32, (rev.shape[0], table.shape[0]), 1) == row
    hot = jnp.where(hot, 1.0, 0.0).astype(jnp.bfloat16)
    got = dot(hot, table)
    return jnp.where(low_lanes(got.shape) != upper, got, 0.0)


EDGE_CHUNK = 512


def mirror_id():
    size = lax.axis_size("cluster")
    return {"cluster": lax.rem(lax.axis_index("cluster") + size // 2, size)}


def narrow_id(slot):
    return {"narrow": slot}


def send(src, dst, send_sem, recv_sem, target):
    return pltpu.make_async_remote_copy(
        src_ref=src,
        dst_ref=dst,
        send_sem=send_sem,
        recv_sem=recv_sem,
        device_id=target,
        device_id_type=pl.DeviceIdType.MESH,
    )


def hello(targets):
    barrier = pltpu.get_barrier_semaphore()
    for t in targets:
        pl.semaphore_signal(barrier, inc=1, device_id=t, device_id_type=pl.DeviceIdType.MESH)
    return lambda: pl.semaphore_wait(barrier, len(targets))


def relayout(ang, amat, tmp, k):
    low = low_lanes((64, 128))
    a = ang[k].astype(jnp.float32)
    for r in range(32):
        t = a[:, 128 * r : 128 * r + 128]
        tmp[16 * r : 16 * r + 8] = t
        tmp[16 * r + 8 : 16 * r + 16] = swap_halves(t)
    for s in range(0, 8, 2):
        first = tmp[pl.ds(s, 64, stride=8), :]
        second = tmp[pl.ds(s + 1, 64, stride=8), :]
        both = jnp.where(low, first, swap_halves(second)).astype(jnp.bfloat16)
        amat[pl.ds(pl.multiple_of(k * 64, 64), 64), s * 64 : s * 64 + 128] = both


def front_kernel(
    src, cnt, x, down, ang,
    mine_out, theirs, pre_out, amat_out,
    xbuf, abuf, trips, amat, pre, mine, rhs, tmp,
    xsem, asem, osem, ysend, yrecv, y2send, y2recv, zsend, zrecv, csend, crecv, msend, mrecv,
):
    row, far, core = place()
    up, dn = slot_of(row + 1, far, core), slot_of(row - 1, far, core)
    anti, sib = slot_of(row, 1 - far, core), slot_of(row, far, 1 - core)
    me = slot_of(row, far, core)
    nbr = (narrow_id(up), narrow_id(dn))
    anti_id, sib_id, mirror = narrow_id(anti), narrow_id(sib), mirror_id()
    group = trips.shape[0] // 16 // CH
    rows = group * 32
    half = {0: (0, 1), 1: (2, 3)}
    wd2 = jnp.concatenate([down[...]] * 2, axis=0)
    loads = []
    for q in range(CH):
        sl = pl.ds(q * 2 * rows, 2 * rows)
        loads.append(pltpu.make_async_copy(x.at[sl], xbuf.at[sl], xsem.at[q]))
        loads[-1].start()
    aload = pltpu.make_async_copy(ang, abuf, asem)
    aload.start()
    arrive = hello((*nbr, anti_id, sib_id, mirror))
    copies = []

    def go(c):
        c.start()
        copies.append(c)
        return c

    def part(slot, q):
        return trips.at[pl.ds((slot * CH + q) * group, group)]

    yc, y2, zc, cc = {}, {}, {}, []
    for q in range(CH):
        loads[q].wait()
        pair = paired(dot_rows(xbuf[q * 2 * rows : (q + 1) * 2 * rows], wd2))
        pre[q * rows : (q + 1) * rows] = pair
        fresh = (pair * sigmoid(pair)).astype(jnp.bfloat16)
        part(me, q)[...] = fresh.reshape(group, 32, 128)
        if q == 0:
            arrive()
        zc[q] = go(send(part(me, q), part(me, q), zsend.at[q], zrecv.at[q], anti_id))
        for d in (0, 1):
            yc[0, d, q] = go(
                send(part(me, q), part(me, q), ysend.at[0, d, q], yrecv.at[0, d, q], nbr[d])
            )
        cc.append(go(send(part(me, q), part(me, q), csend.at[0, q], crecv.at[0, q], sib_id)))
    outs = [pltpu.make_async_copy(pre, pre_out, osem.at[0])]
    outs[0].start()
    aload.wait()
    step = [0]
    blocks_n = amat.shape[0] // 64

    def lay(n):
        lo, hi = step[0], min(step[0] + n, blocks_n)
        step[0] = hi

        def one(k, carry):
            relayout(abuf, amat, tmp, k)
            return carry

        if hi > lo:
            lax.fori_loop(lo, hi, one, 0)

    def came(z, d):
        return slot_of(row - 1 if d == 0 else row + 1, far if z == 0 else 1 - far, core)

    def to_sib(slot, i, q):
        cc.append(go(send(part(slot, q), part(slot, q), csend.at[i, q], crecv.at[i, q], sib_id)))

    def pass_on(z, q):
        for d in (0, 1):
            yc[z, d, q].wait_recv()
            slot = came(z, d)
            if q in half[d]:
                y2[z, q] = go(send(part(slot, q), part(slot, q), y2send.at[z, q], y2recv.at[z, q], nbr[d]))
            to_sib(slot, 1 + z * 4 + d, q)

    def from_far(q):
        zc[q].wait_recv()
        for d in (0, 1):
            yc[1, d, q] = go(
                send(part(anti, q), part(anti, q), ysend.at[1, d, q], yrecv.at[1, d, q], nbr[d])
            )
        to_sib(anti, 3, q)

    def far_row(z, q):
        y2[z, q].wait_recv()
        to_sib(slot_of(row + 2, far if z == 0 else 1 - far, core), 4 if z == 0 else 7, q)

    lay(6)
    pass_on(0, 0)
    lay(4)
    pass_on(0, 1)
    lay(4)
    pass_on(0, 2)
    from_far(0)
    lay(3)
    pass_on(0, 3)
    lay(3)
    from_far(1)
    lay(4)
    far_row(0, 0)
    far_row(0, 2)
    from_far(2)
    lay(4)
    pass_on(1, 0)
    far_row(0, 1)
    far_row(0, 3)
    from_far(3)
    lay(blocks_n)
    outs.append(pltpu.make_async_copy(amat, amat_out, osem.at[1]))
    outs[1].start()
    for q in range(1, CH):
        pass_on(1, q)
    for q in range(CH):
        far_row(1, q)
    for c in cc:
        c.wait_recv()

    per = blocks_n // CH
    mc = []
    for q in range(CH):

        def one(k, carry, q=q):
            used = jnp.broadcast_to(cnt[k], (32, 128))
            for s in range(8):
                v = trips[lax.rem(src[s, k], trips.shape[0])]
                v = jnp.where(used > s, v, jnp.zeros_like(v))
                rhs[s * 64 : s * 64 + 32] = v
                rhs[s * 64 + 32 : s * 64 + 64] = swap_halves(v)
            o = dot(amat[pl.ds(pl.multiple_of(k * 64, 64), 64), :], rhs[...])
            pair = jnp.where(low_lanes((32, 128)), o[:32], swap_halves(o[32:]))
            mine[pl.ds(pl.multiple_of(k * 32, 32), 32), :] = pair.astype(jnp.bfloat16)
            return carry

        lax.fori_loop(q * per, (q + 1) * per, one, 0)
        sl = pl.ds(q * rows, rows)
        mc.append(go(send(mine.at[sl], theirs.at[sl], msend.at[q], mrecv.at[q], mirror)))
    outs.append(pltpu.make_async_copy(mine, mine_out, osem.at[2]))
    outs[2].start()
    for c in mc:
        c.wait_recv()
    for c in copies:
        c.wait_send()
    for c in outs:
        c.wait()


def front(src, cnt, x, down, ang):
    n = x.shape[0]
    dma = pltpu.SemaphoreType.DMA
    vm = pltpu.VMEM
    bf, f32 = jnp.bfloat16, jnp.float32
    anywhere = pl.BlockSpec(memory_space=pl.ANY)
    smem = pl.BlockSpec(memory_space=pltpu.SMEM)
    return pl.pallas_call(
        front_kernel,
        name="front",
        in_specs=[smem, smem, anywhere, pl.BlockSpec(memory_space=vm), anywhere],
        out_specs=[anywhere] * 4,
        out_shape=[
            jax.ShapeDtypeStruct((n // 2, 128), bf),
            jax.ShapeDtypeStruct((n // 2, 128), bf),
            jax.ShapeDtypeStruct((n // 2, 128), f32),
            jax.ShapeDtypeStruct((n, 512), bf),
        ],
        scratch_shapes=[
            vm(x.shape, bf),
            vm(ang.shape, bf),
            vm((n // 4, 32, 128), bf),
            vm((n, 512), bf),
            vm((n // 2, 128), f32),
            vm((n // 2, 128), bf),
            vm((512, 128), bf),
            vm((512, 128), f32),
            dma((CH,)),
            dma,
            dma((3,)),
            dma((2, 2, CH)),
            dma((2, 2, CH)),
            dma((2, CH)),
            dma((2, CH)),
            dma((CH,)),
            dma((CH,)),
            dma((8, CH)),
            dma((8, CH)),
            dma((CH,)),
            dma((CH,)),
        ],
        compiler_params=pltpu.CompilerParams(collective_id=0, has_side_effects=True),
    )(src, cnt, x, down, ang)


def layer_kernel(x, cot, own, theirs, rev, up_w, wi, wo, out, gmsg, got, gown, hs, col, ssem, rsem):
    i = pl.program_id(0)
    mirror = mirror_id()

    @pl.when(i == 0)
    def _():
        hello((mirror,))()
        columns(rev, col)

    c = ROOT_HALF
    w2 = jnp.concatenate([up_w[...]] * 2, axis=0)
    here = pl.ds(pl.multiple_of(i * x.shape[0], x.shape[0]), x.shape[0])
    up, dup = silu_both(dot(spread(own[...]), w2))
    picked = pick_rows(col[here, :], theirs[...]).astype(jnp.bfloat16)
    pup, dpup = silu_both(dot(picked, w2))
    up = up.astype(jnp.bfloat16).astype(jnp.float32)
    pup = pup.astype(jnp.bfloat16).astype(jnp.float32)
    hidden = (x[...].astype(jnp.float32) + (up + pup) * c) * c
    act, dact = silu_both(dot(hidden.astype(jnp.bfloat16), wi[...]))
    res, dres = silu_both(dot(act.astype(jnp.bfloat16), wo[...]))
    out[...] = ((hidden + res) * c).astype(jnp.bfloat16)
    scaled = cot[...].astype(jnp.float32) * c
    grad_out = (scaled * dres).astype(jnp.bfloat16)
    grad_in = (dot_rows(grad_out, wo[...]) * dact).astype(jnp.bfloat16)
    grad_msg = (scaled + dot_rows(grad_in, wi[...])) * c
    gmsg[...] = grad_msg
    rounded = grad_msg.astype(jnp.bfloat16).astype(jnp.float32)
    part = (rounded * (c * dpup)).astype(jnp.bfloat16)
    tile = hs.shape[0] // TILES

    def piece(n):
        sl = pl.ds(pl.multiple_of(n * tile, tile), tile)
        return send(hs.at[sl], got.at[sl], ssem.at[n], rsem.at[n], mirror)

    hs[pl.ds(pl.multiple_of(i * tile, tile), tile), :] = paired(dot_rows(part, w2)).astype(jnp.bfloat16)
    piece(i).start()
    gown[...] = dot_rows((grad_msg * (c * dup)).astype(jnp.bfloat16), w2)

    @pl.when(i == TILES - 1)
    def _():
        for n in range(TILES):
            piece(n).wait()


def layer(x, cot, own, theirs, rev, up, wi, wo):
    n, d = x.shape
    t = n // TILES
    wide = pl.BlockSpec((t, d), lambda i: (i, 0))

    def whole(a):
        return pl.BlockSpec(a.shape, lambda i: (0, 0))

    return pl.pallas_call(
        layer_kernel,
        name="layer",
        grid=(TILES,),
        in_specs=[
            wide,
            wide,
            pl.BlockSpec((t // 2, 128), lambda i: (i, 0)),
            whole(theirs),
            whole(rev),
            whole(up),
            whole(wi),
            whole(wo),
        ],
        out_specs=[
            wide,
            wide,
            pl.BlockSpec(memory_space=pl.ANY),
            pl.BlockSpec((t, 128), lambda i: (i, 0)),
        ],
        out_shape=[
            jax.ShapeDtypeStruct((n, d), jnp.bfloat16),
            jax.ShapeDtypeStruct((n, d), jnp.float32),
            jax.ShapeDtypeStruct((n // 2, 128), jnp.bfloat16),
            jax.ShapeDtypeStruct((n, 128), jnp.float32),
        ],
        scratch_shapes=[
            pltpu.VMEM((n // 2, 128), jnp.bfloat16),
            pltpu.VMEM((n, 1), jnp.int32),
            pltpu.SemaphoreType.DMA((TILES,)),
            pltpu.SemaphoreType.DMA((TILES,)),
        ],
        compiler_params=pltpu.CompilerParams(collective_id=2, has_side_effects=True),
    )(x, cot, own, theirs, rev, up, wi, wo)


def columns(rev, col):
    turned = jnp.transpose(rev[...])
    for j in range(rev.shape[0]):
        col[j * 128 : (j + 1) * 128, :] = turned[:, j : j + 1]


def slot_row(src, cnt):
    slots, n = src.shape
    named = lax.rem(src[...], 512)
    used = lax.broadcasted_iota(jnp.int32, (slots, n), 0) < cnt[...]
    named = jnp.where(used, named, -1).astype(jnp.float32)
    wide = jnp.concatenate([named] * 4, axis=1)
    shape = (slots, 4 * n)
    group = lax.div(lax.broadcasted_iota(jnp.int32, shape, 1), n)
    own = lax.rem(lax.broadcasted_iota(jnp.int32, shape, 0), 4)
    kept = jnp.where(group == own, wide, 0.0)
    halves = [jnp.sum(kept[4 * h : 4 * h + 4], axis=0, keepdims=True) for h in (0, 1)]
    return jnp.concatenate(halves, axis=1)


def back_kernel(
    src, cnt, rev, got, gown, amat,
    out,
    col, pairs, hot, parts, near_buf, y2buf, ybuf, zbuf, stage, acc,
    psend, precv, y2send, y2recv, ysend, yrecv, zsend, zrecv,
):
    row, far, core = place()
    up, dn = slot_of(row + 1, far, core), slot_of(row - 1, far, core)
    anti, sib = slot_of(row, 1 - far, core), slot_of(row, far, 1 - core)
    nbr = (narrow_id(up), narrow_id(dn))
    anti_id, sib_id = narrow_id(anti), narrow_id(sib)
    half = {0: (0, 1), 1: (2, 3)}
    arrive = hello((*nbr, anti_id, sib_id))
    columns(rev, col)

    shape = (512, 256)
    at = lax.broadcasted_iota(jnp.int32, shape, 0)
    named = ((lax.rem(lax.div(at, 32), 4) * 2 + lax.rem(lax.div(at, 128), 2)) * 2 + lax.div(at, 256)) * 32
    named = (named + lax.rem(at, 32)).astype(jnp.float32)
    hot[...] = jnp.where(named == slot_row(src, cnt), 1.0, 0.0).astype(jnp.bfloat16)
    tile = 256

    def tiles(i, carry):
        sl = pl.ds(pl.multiple_of(i * tile, tile), tile)
        theirs = pick_rows(col[sl, :], got[...])
        grad = (gown[sl, :] + theirs + swap_halves(theirs)).astype(jnp.bfloat16)
        for k in range(tile // 64):
            a = amat[pl.ds(pl.multiple_of(i * tile + k * 64, 64), 64), :]
            pair = paired(dot_cols(a, grad[k * 64 : k * 64 + 64]))
            for s in range(8):
                to = pl.multiple_of((s * 32 + i * 4 + k) * 32, 32)
                pairs[pl.ds(to, 32), :] = pair[s * 32 : s * 32 + 32]
        return carry

    lax.fori_loop(0, gown.shape[0] // tile, tiles, 0)
    copies = []

    def go(c):
        c.start()
        copies.append(c)
        return c

    sc, y2, yc, zc = {}, {}, {}, {}
    far_of = (1 - far, far)
    bf = jnp.bfloat16

    def build(q):
        def one(r, carry):
            t = pairs[pl.ds(r, 256, stride=32), :].astype(bf)
            parts[r] = dot(hot[...], t).astype(bf)
            return carry

        lax.fori_loop(8 * q, 8 * q + 8, one, 0)
        sl = pl.ds(8 * q, 8)
        mate = pl.ds(pl.multiple_of((1 - core) * 256, 256), 256)
        sc[q] = go(send(parts.at[sl, mate], near_buf.at[sl], psend.at[q], precv.at[q], sib_id))

    def chip_sum(z, o, q):
        sl = pl.ds(8 * q, 8)
        to = far_of[z] * 128 + lax.rem(row + o, 4) * 32
        a = parts[sl, pl.ds(pl.multiple_of(core * 256 + to, 32), 32), :]
        b = near_buf[sl, pl.ds(pl.multiple_of(to, 32), 32), :]
        return a.astype(jnp.float32) + b.astype(jnp.float32)

    def first(z, q):
        sl = pl.ds(8 * q, 8)
        d = 0 if q in half[0] else 1
        stage[z, 2, sl] = chip_sum(z, 2, q).astype(bf)
        y2[z, q] = go(send(stage.at[z, 2, sl], y2buf.at[z, sl], y2send.at[z, q], y2recv.at[z, q], nbr[d]))
        e = 1 - d
        o = 1 if e == 0 else 3
        stage[z, o, sl] = chip_sum(z, o, q).astype(bf)
        yc[z, e, q] = go(send(stage.at[z, o, sl], ybuf.at[z, e, sl], ysend.at[z, e, q], yrecv.at[z, e, q], nbr[e]))

    def second(z, q):
        sl = pl.ds(8 * q, 8)
        d = 0 if q in half[0] else 1
        o = 1 if d == 0 else 3
        y2[z, q].wait_recv()
        stage[z, o, sl] = (chip_sum(z, o, q) + y2buf[z, sl].astype(jnp.float32)).astype(bf)
        yc[z, d, q] = go(send(stage.at[z, o, sl], ybuf.at[z, d, sl], ysend.at[z, d, q], yrecv.at[z, d, q], nbr[d]))

    def final(z, q):
        sl = pl.ds(8 * q, 8)
        yc[z, 0, q].wait_recv()
        yc[z, 1, q].wait_recv()
        return (
            chip_sum(z, 0, q)
            + ybuf[z, 0, sl].astype(jnp.float32)
            + ybuf[z, 1, sl].astype(jnp.float32)
        )

    order = (0, 2, 1, 3)
    arrive()
    build(order[0])
    for i in range(CH):
        if i + 1 < CH:
            build(order[i + 1])
        sc[order[i]].wait_recv()
        first(0, order[i])
    for q in order:
        second(0, q)
        first(1, q)
    for q in order:
        sl = pl.ds(8 * q, 8)
        stage[0, 0, sl] = final(0, q).astype(bf)
        zc[q] = go(send(stage.at[0, 0, sl], zbuf.at[sl], zsend.at[q], zrecv.at[q], anti_id))
        second(1, q)
    for q in order:
        acc[pl.ds(8 * q, 8)] = final(1, q)
    for q in order:
        sl = pl.ds(8 * q, 8)
        zc[q].wait_recv()
        total = acc[sl] + zbuf[sl].astype(jnp.float32)
        for r in range(8):
            out[pl.ds(8 * q + r, 32, stride=32), :] = total[r]
    for c in copies:
        c.wait_send()


def back(src, cnt, rev, got, gown, amat):
    dma = pltpu.SemaphoreType.DMA
    vm = pltpu.VMEM
    bf, f32 = jnp.bfloat16, jnp.float32
    inside = pl.BlockSpec(memory_space=vm)
    return pl.pallas_call(
        back_kernel,
        name="back",
        in_specs=[inside] * 6,
        out_specs=inside,
        out_shape=jax.ShapeDtypeStruct((1024, 128), f32),
        scratch_shapes=[
            vm((2048, 1), jnp.int32),
            vm((8192, 128), f32),
            vm((512, 256), bf),
            vm((32, 512, 128), bf),
            vm((32, 256, 128), bf),
            vm((2, 32, 32, 128), bf),
            vm((2, 2, 32, 32, 128), bf),
            vm((32, 32, 128), bf),
            vm((2, 4, 32, 32, 128), bf),
            vm((32, 32, 128), f32),
            dma((CH,)),
            dma((CH,)),
            dma((2, CH)),
            dma((2, CH)),
            dma((2, 2, CH)),
            dma((2, 2, CH)),
            dma((CH,)),
            dma((CH,)),
        ],
        compiler_params=pltpu.CompilerParams(collective_id=1, has_side_effects=True),
    )(src, cnt, rev, got, gown, amat)


def last_kernel(gmsg, total, pre, down, res, out, res_out):
    res_out[...] = res[...]
    grad = (total[...] * silu_both(pre[...])[1]).astype(jnp.bfloat16)
    w = jnp.concatenate([down[...]] * 2, axis=0)
    out[...] = (gmsg[...] + dot(spread(grad), w)).astype(jnp.bfloat16)


def last(gmsg, total, pre, down, res):
    n, d = gmsg.shape
    t = n // TILES
    wide = pl.BlockSpec((t, d), lambda i: (i, 0))
    slim = pl.BlockSpec((t // 2, 128), lambda i: (i, 0))
    return pl.pallas_call(
        last_kernel,
        name="last",
        grid=(TILES,),
        in_specs=[wide, slim, slim, pl.BlockSpec(down.shape, lambda i: (0, 0)), wide],
        out_specs=[wide, wide],
        out_shape=[jax.ShapeDtypeStruct((n, d), jnp.bfloat16)] * 2,
    )(gmsg, total, pre, down, res)


def on_device(x, cot, down, up, inner, outer, ang, reverse, sources, counts):
    down, src = down.T, sources.T
    rev = reverse.reshape(-1, 128)
    own, theirs, pre, amat = front(src, counts, x, down, ang)
    res, gmsg, got, gown = layer(x, cot, own, theirs, rev, up, inner[0], outer[0])
    total = back(src, counts.reshape(1, -1), rev, got, gown, amat)
    grad_x, out = last(gmsg, total, pre, down, res)
    return out, grad_x


def solution(mesh):
    rows = P(("cluster", "narrow"))
    specs = (rows, rows, P(), P(), P(), P(), rows, rows, rows, rows)
    return jax.shard_map(
        on_device, mesh=mesh, in_specs=specs, out_specs=(rows, rows), check_vma=False
    )
```

time: 370 us -> 127 us (0.34)
  waiting for transfers between devices: 184 us -> 0 us
  Pallas kernels: 0 us -> 127 us
  blocking collectives: 57.4 us -> 0 us
  local copies, waits for them, and re-layouts: 53.4 us -> 0 us
  matrix products: 52 us -> 0 us
  between operations: 14.3 us -> 0.65 us
  other arithmetic: 8.01 us -> 0 us
    pallas_call x0 -> x4, Pallas kernels: none -> 127 us  [the longest x1 49.6 us: front(): pl.pallas_call(front_kernel, name='front', in_specs=[smem, smem, anywhere...]
    ppermute x2 -> x0, waiting for transfers between devices: 108 us -> none  [swapped(): lax.ppermute(array, axis, [(i, i ^ 1 << bit) for i in range(lax.axis_size...]
    all_gather x1 -> x0, waiting for transfers between devices: 75.6 us -> none  [on_device(): shard_piece = lax.all_gather(trip_blocks, 'narrow', axis=0, tiled=True)]
    all_to_all x1 -> x0, blocking collectives: 57.4 us -> none  [side_by_side(): lax.all_to_all(both, axis, split_axis=split_dim, concat_axis=concat_dim,...]
    dot_general x13 -> x0, matrix products: 52 us -> none  [the longest x3 20.3 us: dot_trans(): lax.dot_general(operand, matrix, (((1,), (1,)), ((), ())), preferred_elem...]
    reshape x9 -> x0, local copies, waits for them, and re-layouts: 21.6 us -> none  [the longest x1 7.9 us: on_device(): pair_terms.reshape(local_blocks, slot_count, block_edges * trip_width)]
    gather x4 -> x0, local copies, waits for them, and re-layouts: 20.5 us -> none  [the longest x1 9.2 us: on_device(): partner_grad = swapped(grad_msg_round, 'cluster', top_bit)[rev_slot]]
    dot_general x1 -> x0, local copies, waits for them, and re-layouts: 8.99 us -> none  [on_device(): jnp.einsum('ksij,kif->ksjf', angle_mats, grad_blocks, preferred_element_t...]
  transfers between devices with their start and end apart: 3 -> 0, of which waited for: 3 -> 0; matrix products, arithmetic and copies ran while one was open for 4% -> 0% of each run, Pallas kernels for 0% -> 0%
where the time goes in v3:
time: 127 us
  Pallas kernels  127 us (100%)
    pallas_call x1, Pallas kernels, front(): pl.pallas_call(front_kernel, name='front', in_specs=[smem, smem, anywhere...  49.6 us
    pallas_call x1, Pallas kernels, back(): pl.pallas_call(back_kernel, name='back', in_specs=[inside] * 6, out_specs...  45 us
    pallas_call x1, Pallas kernels, layer(): pl.pallas_call(layer_kernel, name='layer', grid=(TILES,), in_specs=[wide,...  24.3 us
    pallas_call x1, Pallas kernels, last(): pl.pallas_call(last_kernel, name='last', grid=(TILES,), in_specs=[wide, s...  7.55 us

profile of v3, /device:TPU:1, one launch (start us, length us, event | category | flops | bytes accessed | tf_op | source)
XLA Modules:
  0.0 127.2 jit_solution(17090153061303683198)
XLA Ops:
  0.6 49.6 %front.1 = (bf16[1024,128]{1,0:T(8,128)(2,1)}, bf16[1024,128]{1,0:T(8,128)(2,1)}, f32[1024,128]{1,0:T(8,128)}, bf16[2048,512]{1,0:T(8,128)(2,1)}) custom-call(s32[8,32]{1,0:T(8,128)} %bitcast.12, s32[32]{0:T(128)} %cnt.1, bf16[2048,512]{1,0:T(8,128)(2,1)} %x.3, bf16[64,512]{1,0:T(8,128)(2,1)} %bitcast.8, bf16[32,8,4096]{2,1,0:T(8,128)(2,1)} %ang.1), custom_call_target="tpu_custom_call" | custom-call | tf_op jit(solution)/shard_map/front/pallas_call | solution.py:286
  50.2 24.3 %layer.1 = (bf16[2048,512]{1,0:T(8,128)(2,1)}, f32[2048,512]{1,0:T(8,128)}, bf16[1024,128]{1,0:T(8,128)(2,1)}, f32[2048,128]{1,0:T(8,128)}) custom-call(bf16[2048,512]{1,0:T(8,128)(2,1)} %x.3, bf16[2048,512]{1,0:T(8,128)(2,1)} %cot.1, bf16[1024,128]{1,0:T(8,128)(2,1)} %get-tuple-element.12.own, bf16[1024,128]{1,0:T(8,128)(2,1)} %get-tuple-element.13.theirs, ...), custom_call_target="tpu_custom_call" | custom-call | tf_op jit(solution)/shard_map/layer/pallas_call | solution.py:376
  74.6 45.0 %back.1.total = f32[1024,128]{1,0:T(8,128)} custom-call(s32[8,32]{1,0:T(8,128)} %bitcast.13, s32[1,32]{1,0:T(1,128)} %bitcast.14, s32[16,128]{1,0:T(8,128)} %bitcast.11, bf16[1024,128]{1,0:T(8,128)(2,1)} %get-tuple-element.15.got, f32[2048,128]{1,0:T(8,128)} %get-tuple-element.16.gown, bf16[2048,512]{1,0:T(8,128)(2,1)} %get-tuple-element.17.amat), custom_call_target="tpu_custom_call" | custom-call | tf_op jit(solution)/shard_map/back/pallas_call | solution.py:557
  119.6 7.5 %last.1 = (bf16[2048,512]{1,0:T(8,128)(2,1)}, bf16[2048,512]{1,0:T(8,128)(2,1)}) custom-call(f32[2048,512]{1,0:T(8,128)} %get-tuple-element.14.gmsg, f32[1024,128]{1,0:T(8,128)} %back.1.total, f32[1024,128]{1,0:T(8,128)} %get-tuple-element.18.pre, bf16[64,512]{1,0:T(8,128)(2,1)} %bitcast.9, bf16[2048,512]{1,0:T(8,128)(2,1)} %get-tuple-element.19.res), custom_call_target="tpu_custom_call" | custom-call | tf_op jit(solution)/shard_map/last/pallas_call | solution.py:599

commit v4 on v3

--- a/solution.py
+++ b/solution.py
@@ -23,6 +23,7 @@
 
 ROOT_HALF = 0.7071067811865476
 TILES = 8
+LAST_TILES = 4
 
 
 def sigmoid(v):
@@ -126,10 +127,10 @@
 
 
 def front_kernel(
-    src, cnt, x, down, ang,
-    mine_out, theirs, pre_out, amat_out,
-    xbuf, abuf, trips, amat, pre, mine, rhs, tmp,
-    xsem, asem, osem, ysend, yrecv, y2send, y2recv, zsend, zrecv, csend, crecv, msend, mrecv,
+    src, cnt, x, down, up_w, ang,
+    theirs, pre_out, amat_out, up_out, slope_out,
+    xbuf, abuf, trips, amat, pre, mine, rhs, tmp, ups, slopes,
+    xsem, asem, osem, usem, ysend, yrecv, y2send, y2recv, zsend, zrecv, csend, crecv, msend, mrecv,
 ):
     row, far, core = place()
     up, dn = slot_of(row + 1, far, core), slot_of(row - 1, far, core)
@@ -266,8 +267,22 @@
         lax.fori_loop(q * per, (q + 1) * per, one, 0)
         sl = pl.ds(q * rows, rows)
         mc.append(go(send(mine.at[sl], theirs.at[sl], msend.at[q], mrecv.at[q], mirror)))
-    outs.append(pltpu.make_async_copy(mine, mine_out, osem.at[2]))
-    outs[2].start()
+    w2 = jnp.concatenate([up_w[...]] * 2, axis=0)
+    for q in range(CH):
+
+        def raise_tile(i, carry):
+            own = mine[pl.ds(pl.multiple_of(i * 128, 128), 128), :]
+            value, slope = silu_both(dot(spread(own), w2))
+            sl = pl.ds(pl.multiple_of(i * 256, 256), 256)
+            ups[sl, :] = value.astype(jnp.bfloat16)
+            slopes[sl, :] = slope.astype(jnp.bfloat16)
+            return carry
+
+        lax.fori_loop(q * rows // 128, (q + 1) * rows // 128, raise_tile, 0)
+        sl = pl.ds(q * 2 * rows, 2 * rows)
+        for j, (a, b) in enumerate(((ups, up_out), (slopes, slope_out))):
+            outs.append(pltpu.make_async_copy(a.at[sl], b.at[sl], usem.at[j, q]))
+            outs[-1].start()
     for c in mc:
         c.wait_recv()
     for c in copies:
@@ -276,7 +291,7 @@
         c.wait()
 
 
-def front(src, cnt, x, down, ang):
+def front(src, cnt, x, down, up, ang):
     n = x.shape[0]
     dma = pltpu.SemaphoreType.DMA
     vm = pltpu.VMEM
@@ -286,12 +301,13 @@
     return pl.pallas_call(
         front_kernel,
         name="front",
-        in_specs=[smem, smem, anywhere, pl.BlockSpec(memory_space=vm), anywhere],
-        out_specs=[anywhere] * 4,
+        in_specs=[smem, smem, anywhere] + [pl.BlockSpec(memory_space=vm)] * 2 + [anywhere],
+        out_specs=[anywhere] * 5,
         out_shape=[
             jax.ShapeDtypeStruct((n // 2, 128), bf),
-            jax.ShapeDtypeStruct((n // 2, 128), bf),
             jax.ShapeDtypeStruct((n // 2, 128), f32),
+            jax.ShapeDtypeStruct((n, 512), bf),
+            jax.ShapeDtypeStruct((n, 512), bf),
             jax.ShapeDtypeStruct((n, 512), bf),
         ],
         scratch_shapes=[
@@ -303,9 +319,12 @@
             vm((n // 2, 128), bf),
             vm((512, 128), bf),
             vm((512, 128), f32),
+            vm((n, 512), bf),
+            vm((n, 512), bf),
             dma((CH,)),
             dma,
-            dma((3,)),
+            dma((2,)),
+            dma((2, CH)),
             dma((2, 2, CH)),
             dma((2, 2, CH)),
             dma((2, CH)),
@@ -318,10 +337,10 @@
             dma((CH,)),
         ],
         compiler_params=pltpu.CompilerParams(collective_id=0, has_side_effects=True),
-    )(src, cnt, x, down, ang)
-
-
-def layer_kernel(x, cot, own, theirs, rev, up_w, wi, wo, out, gmsg, got, gown, hs, col, ssem, rsem):
+    )(src, cnt, x, down, up, ang)
+
+
+def layer_kernel(x, cot, ups, slopes, theirs, rev, up_w, wi, wo, out, gmsg, got, gown, hs, col, ssem, rsem):
     i = pl.program_id(0)
     mirror = mirror_id()
 
@@ -333,10 +352,9 @@
     c = ROOT_HALF
     w2 = jnp.concatenate([up_w[...]] * 2, axis=0)
     here = pl.ds(pl.multiple_of(i * x.shape[0], x.shape[0]), x.shape[0])
-    up, dup = silu_both(dot(spread(own[...]), w2))
+    up, dup = ups[...].astype(jnp.float32), slopes[...].astype(jnp.float32)
     picked = pick_rows(col[here, :], theirs[...]).astype(jnp.bfloat16)
     pup, dpup = silu_both(dot(picked, w2))
-    up = up.astype(jnp.bfloat16).astype(jnp.float32)
     pup = pup.astype(jnp.bfloat16).astype(jnp.float32)
     hidden = (x[...].astype(jnp.float32) + (up + pup) * c) * c
     act, dact = silu_both(dot(hidden.astype(jnp.bfloat16), wi[...]))
@@ -346,7 +364,7 @@
     grad_out = (scaled * dres).astype(jnp.bfloat16)
     grad_in = (dot_rows(grad_out, wo[...]) * dact).astype(jnp.bfloat16)
     grad_msg = (scaled + dot_rows(grad_in, wi[...])) * c
-    gmsg[...] = grad_msg
+    gmsg[...] = grad_msg.astype(jnp.bfloat16)
     rounded = grad_msg.astype(jnp.bfloat16).astype(jnp.float32)
     part = (rounded * (c * dpup)).astype(jnp.bfloat16)
     tile = hs.shape[0] // TILES
@@ -365,7 +383,7 @@
             piece(n).wait()
 
 
-def layer(x, cot, own, theirs, rev, up, wi, wo):
+def layer(x, cot, ups, slopes, theirs, rev, up, wi, wo):
     n, d = x.shape
     t = n // TILES
     wide = pl.BlockSpec((t, d), lambda i: (i, 0))
@@ -380,7 +398,8 @@
         in_specs=[
             wide,
             wide,
-            pl.BlockSpec((t // 2, 128), lambda i: (i, 0)),
+            wide,
+            wide,
             whole(theirs),
             whole(rev),
             whole(up),
@@ -395,7 +414,7 @@
         ],
         out_shape=[
             jax.ShapeDtypeStruct((n, d), jnp.bfloat16),
-            jax.ShapeDtypeStruct((n, d), jnp.float32),
+            jax.ShapeDtypeStruct((n, d), jnp.bfloat16),
             jax.ShapeDtypeStruct((n // 2, 128), jnp.bfloat16),
             jax.ShapeDtypeStruct((n, 128), jnp.float32),
         ],
@@ -406,7 +425,7 @@
             pltpu.SemaphoreType.DMA((TILES,)),
         ],
         compiler_params=pltpu.CompilerParams(collective_id=2, has_side_effects=True),
-    )(x, cot, own, theirs, rev, up, wi, wo)
+    )(x, cot, ups, slopes, theirs, rev, up, wi, wo)
 
 
 def columns(rev, col):
@@ -476,12 +495,14 @@
     bf = jnp.bfloat16
 
     def build(q):
-        def one(r, carry):
-            t = pairs[pl.ds(r, 256, stride=32), :].astype(bf)
-            parts[r] = dot(hot[...], t).astype(bf)
+        def one(g, carry):
+            t = [pairs[pl.ds(g * 2 + e, 256, stride=32), :].astype(bf) for e in (0, 1)]
+            both = dot(hot[...], jnp.concatenate(t, axis=1)).astype(bf)
+            for e in (0, 1):
+                parts[g * 2 + e] = both[:, e * 128 : e * 128 + 128]
             return carry
 
-        lax.fori_loop(8 * q, 8 * q + 8, one, 0)
+        lax.fori_loop(4 * q, 4 * q + 4, one, 0)
         sl = pl.ds(8 * q, 8)
         mate = pl.ds(pl.multiple_of((1 - core) * 256, 256), 256)
         sc[q] = go(send(parts.at[sl, mate], near_buf.at[sl], psend.at[q], precv.at[q], sib_id))
@@ -588,18 +609,18 @@
     res_out[...] = res[...]
     grad = (total[...] * silu_both(pre[...])[1]).astype(jnp.bfloat16)
     w = jnp.concatenate([down[...]] * 2, axis=0)
-    out[...] = (gmsg[...] + dot(spread(grad), w)).astype(jnp.bfloat16)
+    out[...] = (gmsg[...].astype(jnp.float32) + dot(spread(grad), w)).astype(jnp.bfloat16)
 
 
 def last(gmsg, total, pre, down, res):
     n, d = gmsg.shape
-    t = n // TILES
+    t = n // LAST_TILES
     wide = pl.BlockSpec((t, d), lambda i: (i, 0))
     slim = pl.BlockSpec((t // 2, 128), lambda i: (i, 0))
     return pl.pallas_call(
         last_kernel,
         name="last",
-        grid=(TILES,),
+        grid=(LAST_TILES,),
         in_specs=[wide, slim, slim, pl.BlockSpec(down.shape, lambda i: (0, 0)), wide],
         out_specs=[wide, wide],
         out_shape=[jax.ShapeDtypeStruct((n, d), jnp.bfloat16)] * 2,
@@ -609,8 +630,8 @@
 def on_device(x, cot, down, up, inner, outer, ang, reverse, sources, counts):
     down, src = down.T, sources.T
     rev = reverse.reshape(-1, 128)
-    own, theirs, pre, amat = front(src, counts, x, down, ang)
-    res, gmsg, got, gown = layer(x, cot, own, theirs, rev, up, inner[0], outer[0])
+    theirs, pre, amat, ups, slopes = front(src, counts, x, down, up, ang)
+    res, gmsg, got, gown = layer(x, cot, ups, slopes, theirs, rev, up, inner[0], outer[0])
     total = back(src, counts.reshape(1, -1), rev, got, gown, amat)
     grad_x, out = last(gmsg, total, pre, down, res)
     return out, grad_x

time: 127 us -> 119 us (0.937)
  Pallas kernels: 127 us -> 118 us
    pallas_call x1, Pallas kernels: 45 us -> 39 us  [back(): pl.pallas_call(back_kernel, name='back', in_specs=[inside] * 6, out_specs...]
    pallas_call x1, Pallas kernels: 7.55 us -> 5.32 us  [last(): pl.pallas_call(last_kernel, name='last', grid=(LAST_TILES,), in_specs=[wi...]
where the time goes in v4:
time: 119 us; the launch traced here: 118 us
  Pallas kernels  118 us (99%)
    pallas_call x1, Pallas kernels, front(): pl.pallas_call(front_kernel, name='front', in_specs=[smem, smem, anywhere...  49.7 us
    pallas_call x1, Pallas kernels, back(): pl.pallas_call(back_kernel, name='back', in_specs=[inside] * 6, out_specs...  39 us
    pallas_call x1, Pallas kernels, layer(): pl.pallas_call(layer_kernel, name='layer', grid=(TILES,), in_specs=[wide,...  23.6 us
    pallas_call x1, Pallas kernels, last(): pl.pallas_call(last_kernel, name='last', grid=(LAST_TILES,), in_specs=[wi...  5.32 us

profile of v4, /device:TPU:1, one launch (start us, length us, event | category | flops | bytes accessed | tf_op | source)
XLA Modules:
  0.0 118.3 jit_solution(11891706963365724292)
XLA Ops:
  0.6 49.7 %front.1 = (bf16[1024,128]{1,0:T(8,128)(2,1)}, f32[1024,128]{1,0:T(8,128)}, bf16[2048,512]{1,0:T(8,128)(2,1)}, bf16[2048,512]{1,0:T(8,128)(2,1)}, bf16[2048,512]{1,0:T(8,128)(2,1)}) custom-call(s32[8,32]{1,0:T(8,128)} %bitcast.12, s32[32]{0:T(128)} %cnt.1, bf16[2048,512]{1,0:T(8,128)(2,1)} %x.3, bf16[64,512]{1,0:T(8,128)(2,1)} %bitcast.8, ...), custom_call_target="tpu_custom_call" | custom-call | tf_op jit(solution)/shard_map/front/pallas_call | solution.py:301
  50.3 23.6 %layer.1 = (bf16[2048,512]{1,0:T(8,128)(2,1)}, bf16[2048,512]{1,0:T(8,128)(2,1)}, bf16[1024,128]{1,0:T(8,128)(2,1)}, f32[2048,128]{1,0:T(8,128)}) custom-call(bf16[2048,512]{1,0:T(8,128)(2,1)} %x.3, bf16[2048,512]{1,0:T(8,128)(2,1)} %cot.1, bf16[2048,512]{1,0:T(8,128)(2,1)} %get-tuple-element.13.ups, bf16[2048,512]{1,0:T(8,128)(2,1)} %get-tuple-element.14.slopes, ...), custom_call_target="tpu_custom_call" | custom-call | tf_op jit(solution)/shard_map/layer/pallas_call | solution.py:394
  74.0 39.0 %back.1.total = f32[1024,128]{1,0:T(8,128)} custom-call(s32[8,32]{1,0:T(8,128)} %bitcast.13, s32[1,32]{1,0:T(1,128)} %bitcast.14, s32[16,128]{1,0:T(8,128)} %bitcast.11, bf16[1024,128]{1,0:T(8,128)(2,1)} %get-tuple-element.17.got, f32[2048,128]{1,0:T(8,128)} %get-tuple-element.18.gown, bf16[2048,512]{1,0:T(8,128)(2,1)} %get-tuple-element.19.amat), custom_call_target="tpu_custom_call" | custom-call | tf_op jit(solution)/shard_map/back/pallas_call | solution.py:578
  113.0 5.3 %last.1 = (bf16[2048,512]{1,0:T(8,128)(2,1)}, bf16[2048,512]{1,0:T(8,128)(2,1)}) custom-call(bf16[2048,512]{1,0:T(8,128)(2,1)} %get-tuple-element.16.gmsg, f32[1024,128]{1,0:T(8,128)} %back.1.total, f32[1024,128]{1,0:T(8,128)} %get-tuple-element.20.pre, bf16[64,512]{1,0:T(8,128)(2,1)} %bitcast.9, bf16[2048,512]{1,0:T(8,128)(2,1)} %get-tuple-element.21.res), custom_call_target="tpu_custom_call" | custom-call | tf_op jit(solution)/shard_map/last/pallas_call | solution.py:620

commit v5 on v4

--- a/solution.py
+++ b/solution.py
@@ -22,7 +22,7 @@
 
 
 ROOT_HALF = 0.7071067811865476
-TILES = 8
+LAYER_TILES = 4
 LAST_TILES = 4
 
 
@@ -76,9 +76,15 @@
     block, rest = lax.div(edge, 64), lax.rem(edge, 64)
     row = block * 32 + lax.rem(rest, 32)
     upper = rest >= 32
-    hot = lax.broadcasted_iota(jnp.int32, (rev.shape[0], table.shape[0]), 1) == row
+    part = table.shape[0] // 4
+    inner, outer = lax.rem(row, part), lax.div(row, part)
+    hot = lax.broadcasted_iota(jnp.int32, (rev.shape[0], part), 1) == inner
     hot = jnp.where(hot, 1.0, 0.0).astype(jnp.bfloat16)
-    got = dot(hot, table)
+    wide = jnp.concatenate([table[j * part : (j + 1) * part] for j in range(4)], axis=1)
+    four = dot(hot, wide)
+    got = four[:, :128]
+    for j in range(1, 4):
+        got = jnp.where(outer == j, four[:, j * 128 : j * 128 + 128], got)
     return jnp.where(low_lanes(got.shape) != upper, got, 0.0)
 
 
@@ -252,19 +258,23 @@
     mc = []
     for q in range(CH):
 
-        def one(k, carry, q=q):
-            used = jnp.broadcast_to(cnt[k], (32, 128))
-            for s in range(8):
-                v = trips[lax.rem(src[s, k], trips.shape[0])]
-                v = jnp.where(used > s, v, jnp.zeros_like(v))
-                rhs[s * 64 : s * 64 + 32] = v
-                rhs[s * 64 + 32 : s * 64 + 64] = swap_halves(v)
-            o = dot(amat[pl.ds(pl.multiple_of(k * 64, 64), 64), :], rhs[...])
-            pair = jnp.where(low_lanes((32, 128)), o[:32], swap_halves(o[32:]))
-            mine[pl.ds(pl.multiple_of(k * 32, 32), 32), :] = pair.astype(jnp.bfloat16)
+        def one(p, carry, q=q):
+            for e in (0, 1):
+                k = p * 2 + e
+                used = jnp.broadcast_to(cnt[k], (32, 128))
+                for s in range(8):
+                    v = trips[lax.rem(src[s, k], trips.shape[0])]
+                    v = jnp.where(used > s, v, jnp.zeros_like(v))
+                    rhs[e, s * 64 : s * 64 + 32] = v
+                    rhs[e, s * 64 + 32 : s * 64 + 64] = swap_halves(v)
+            for e in (0, 1):
+                k = p * 2 + e
+                o = dot(amat[pl.ds(pl.multiple_of(k * 64, 64), 64), :], rhs[e])
+                pair = jnp.where(low_lanes((32, 128)), o[:32], swap_halves(o[32:]))
+                mine[pl.ds(pl.multiple_of(k * 32, 32), 32), :] = pair.astype(jnp.bfloat16)
             return carry
 
-        lax.fori_loop(q * per, (q + 1) * per, one, 0)
+        lax.fori_loop(q * per // 2, (q + 1) * per // 2, one, 0)
         sl = pl.ds(q * rows, rows)
         mc.append(go(send(mine.at[sl], theirs.at[sl], msend.at[q], mrecv.at[q], mirror)))
     w2 = jnp.concatenate([up_w[...]] * 2, axis=0)
@@ -317,7 +327,7 @@
             vm((n, 512), bf),
             vm((n // 2, 128), f32),
             vm((n // 2, 128), bf),
-            vm((512, 128), bf),
+            vm((2, 512, 128), bf),
             vm((512, 128), f32),
             vm((n, 512), bf),
             vm((n, 512), bf),
@@ -367,7 +377,7 @@
     gmsg[...] = grad_msg.astype(jnp.bfloat16)
     rounded = grad_msg.astype(jnp.bfloat16).astype(jnp.float32)
     part = (rounded * (c * dpup)).astype(jnp.bfloat16)
-    tile = hs.shape[0] // TILES
+    tile = hs.shape[0] // LAYER_TILES
 
     def piece(n):
         sl = pl.ds(pl.multiple_of(n * tile, tile), tile)
@@ -377,15 +387,15 @@
     piece(i).start()
     gown[...] = dot_rows((grad_msg * (c * dup)).astype(jnp.bfloat16), w2)
 
-    @pl.when(i == TILES - 1)
+    @pl.when(i == LAYER_TILES - 1)
     def _():
-        for n in range(TILES):
+        for n in range(LAYER_TILES):
             piece(n).wait()
 
 
 def layer(x, cot, ups, slopes, theirs, rev, up, wi, wo):
     n, d = x.shape
-    t = n // TILES
+    t = n // LAYER_TILES
     wide = pl.BlockSpec((t, d), lambda i: (i, 0))
 
     def whole(a):
@@ -394,7 +404,7 @@
     return pl.pallas_call(
         layer_kernel,
         name="layer",
-        grid=(TILES,),
+        grid=(LAYER_TILES,),
         in_specs=[
             wide,
             wide,
@@ -421,8 +431,8 @@
         scratch_shapes=[
             pltpu.VMEM((n // 2, 128), jnp.bfloat16),
             pltpu.VMEM((n, 1), jnp.int32),
-            pltpu.SemaphoreType.DMA((TILES,)),
-            pltpu.SemaphoreType.DMA((TILES,)),
+            pltpu.SemaphoreType.DMA((LAYER_TILES,)),
+            pltpu.SemaphoreType.DMA((LAYER_TILES,)),
         ],
         compiler_params=pltpu.CompilerParams(collective_id=2, has_side_effects=True),
     )(x, cot, ups, slopes, theirs, rev, up, wi, wo)
@@ -449,9 +459,9 @@
 
 
 def back_kernel(
-    src, cnt, rev, got, gown, amat,
+    src, cnt, rev, got, gown_in, amat_in,
     out,
-    col, pairs, hot, parts, near_buf, y2buf, ybuf, zbuf, stage, acc,
+    gown, amat, lsem, col, pairs, hot, parts, near_buf, y2buf, ybuf, zbuf, stage, acc,
     psend, precv, y2send, y2recv, ysend, yrecv, zsend, zrecv,
 ):
     row, far, core = place()
@@ -461,6 +471,12 @@
     anti_id, sib_id = narrow_id(anti), narrow_id(sib)
     half = {0: (0, 1), 1: (2, 3)}
     arrive = hello((*nbr, anti_id, sib_id))
+    loads = [
+        pltpu.make_async_copy(gown_in, gown, lsem.at[0]),
+        pltpu.make_async_copy(amat_in, amat, lsem.at[1]),
+    ]
+    for c in loads:
+        c.start()
     columns(rev, col)
 
     shape = (512, 256)
@@ -468,7 +484,7 @@
     named = ((lax.rem(lax.div(at, 32), 4) * 2 + lax.rem(lax.div(at, 128), 2)) * 2 + lax.div(at, 256)) * 32
     named = (named + lax.rem(at, 32)).astype(jnp.float32)
     hot[...] = jnp.where(named == slot_row(src, cnt), 1.0, 0.0).astype(jnp.bfloat16)
-    tile = 256
+    tile = 512
 
     def tiles(i, carry):
         sl = pl.ds(pl.multiple_of(i * tile, tile), tile)
@@ -478,10 +494,12 @@
             a = amat[pl.ds(pl.multiple_of(i * tile + k * 64, 64), 64), :]
             pair = paired(dot_cols(a, grad[k * 64 : k * 64 + 64]))
             for s in range(8):
-                to = pl.multiple_of((s * 32 + i * 4 + k) * 32, 32)
+                to = pl.multiple_of((s * 32 + i * (tile // 64) + k) * 32, 32)
                 pairs[pl.ds(to, 32), :] = pair[s * 32 : s * 32 + 32]
         return carry
 
+    for c in loads:
+        c.wait()
     lax.fori_loop(0, gown.shape[0] // tile, tiles, 0)
     copies = []
 
@@ -578,10 +596,13 @@
     return pl.pallas_call(
         back_kernel,
         name="back",
-        in_specs=[inside] * 6,
+        in_specs=[inside] * 4 + [pl.BlockSpec(memory_space=pl.ANY)] * 2,
         out_specs=inside,
         out_shape=jax.ShapeDtypeStruct((1024, 128), f32),
         scratch_shapes=[
+            vm(gown.shape, f32),
+            vm(amat.shape, bf),
+            dma((2,)),
             vm((2048, 1), jnp.int32),
             vm((8192, 128), f32),
             vm((512, 256), bf),

time: 119 us -> 115 us (0.966)
  Pallas kernels: 118 us -> 114 us
    pallas_call x2, Pallas kernels: 62.6 us -> 59.7 us  [the longest x1 38.4 us: back(): pl.pallas_call(back_kernel, name='back', in_specs=[inside] * 4 + [pl.Bloc...]
where the time goes in v5:
time: 115 us; the launch traced here: 114 us
  Pallas kernels  114 us (99%)
    pallas_call x1, Pallas kernels, front(): pl.pallas_call(front_kernel, name='front', in_specs=[smem, smem, anywhere...  48.6 us
    pallas_call x1, Pallas kernels, back(): pl.pallas_call(back_kernel, name='back', in_specs=[inside] * 4 + [pl.Bloc...  38.4 us
    pallas_call x1, Pallas kernels, layer(): pl.pallas_call(layer_kernel, name='layer', grid=(LAYER_TILES,), in_specs=...  21.3 us
    pallas_call x1, Pallas kernels, last(): pl.pallas_call(last_kernel, name='last', grid=(LAST_TILES,), in_specs=[wi...  5.32 us

profile of v5, /device:TPU:1, one launch (start us, length us, event | category | flops | bytes accessed | tf_op | source)
XLA Modules:
  0.0 114.3 jit_solution(16940085611093076544)
XLA Ops:
  0.6 48.6 %front.1 = (bf16[1024,128]{1,0:T(8,128)(2,1)}, f32[1024,128]{1,0:T(8,128)}, bf16[2048,512]{1,0:T(8,128)(2,1)}, bf16[2048,512]{1,0:T(8,128)(2,1)}, bf16[2048,512]{1,0:T(8,128)(2,1)}) custom-call(s32[8,32]{1,0:T(8,128)} %bitcast.12, s32[32]{0:T(128)} %cnt.1, bf16[2048,512]{1,0:T(8,128)(2,1)} %x.3, bf16[64,512]{1,0:T(8,128)(2,1)} %bitcast.8, ...), custom_call_target="tpu_custom_call" | custom-call | tf_op jit(solution)/shard_map/front/pallas_call | solution.py:311
  49.3 21.3 %layer.1 = (bf16[2048,512]{1,0:T(8,128)(2,1)}, bf16[2048,512]{1,0:T(8,128)(2,1)}, bf16[1024,128]{1,0:T(8,128)(2,1)}, f32[2048,128]{1,0:T(8,128)}) custom-call(bf16[2048,512]{1,0:T(8,128)(2,1)} %x.3, bf16[2048,512]{1,0:T(8,128)(2,1)} %cot.1, bf16[2048,512]{1,0:T(8,128)(2,1)} %get-tuple-element.13.ups, bf16[2048,512]{1,0:T(8,128)(2,1)} %get-tuple-element.14.slopes, ...), custom_call_target="tpu_custom_call" | custom-call | tf_op jit(solution)/shard_map/layer/pallas_call | solution.py:404
  70.6 38.4 %back.1.total = f32[1024,128]{1,0:T(8,128)} custom-call(s32[8,32]{1,0:T(8,128)} %bitcast.13, s32[1,32]{1,0:T(1,128)} %bitcast.14, s32[16,128]{1,0:T(8,128)} %bitcast.11, bf16[1024,128]{1,0:T(8,128)(2,1)} %get-tuple-element.17.got, f32[2048,128]{1,0:T(8,128)} %get-tuple-element.18.gown_in, bf16[2048,512]{1,0:T(8,128)(2,1)} %get-tuple-element.19.amat_in), custom_call_target="tpu_custom_call" | custom-call | tf_op jit(solution)/shard_map/back/pallas_call | solution.py:596
  109.0 5.3 %last.1 = (bf16[2048,512]{1,0:T(8,128)(2,1)}, bf16[2048,512]{1,0:T(8,128)(2,1)}) custom-call(bf16[2048,512]{1,0:T(8,128)(2,1)} %get-tuple-element.16.gmsg, f32[1024,128]{1,0:T(8,128)} %back.1.total, f32[1024,128]{1,0:T(8,128)} %get-tuple-element.20.pre, bf16[64,512]{1,0:T(8,128)(2,1)} %bitcast.9, bf16[2048,512]{1,0:T(8,128)(2,1)} %get-tuple-element.21.res), custom_call_target="tpu_custom_call" | custom-call | tf_op jit(solution)/shard_map/last/pallas_call | solution.py:641

commit v6 on v5

--- a/solution.py
+++ b/solution.py
@@ -7,6 +7,7 @@
 from jax.sharding import PartitionSpec as P
 
 CH = 4
+MIRROR_PARTS = 8
 
 
 def place():
@@ -254,9 +255,10 @@
     for c in cc:
         c.wait_recv()
 
-    per = blocks_n // CH
+    per = blocks_n // MIRROR_PARTS
+    span = mine.shape[0] // MIRROR_PARTS
     mc = []
-    for q in range(CH):
+    for q in range(MIRROR_PARTS):
 
         def one(p, carry, q=q):
             for e in (0, 1):
@@ -275,7 +277,7 @@
             return carry
 
         lax.fori_loop(q * per // 2, (q + 1) * per // 2, one, 0)
-        sl = pl.ds(q * rows, rows)
+        sl = pl.ds(q * span, span)
         mc.append(go(send(mine.at[sl], theirs.at[sl], msend.at[q], mrecv.at[q], mirror)))
     w2 = jnp.concatenate([up_w[...]] * 2, axis=0)
     for q in range(CH):
@@ -343,8 +345,8 @@
             dma((CH,)),
             dma((8, CH)),
             dma((8, CH)),
-            dma((CH,)),
-            dma((CH,)),
+            dma((MIRROR_PARTS,)),
+            dma((MIRROR_PARTS,)),
         ],
         compiler_params=pltpu.CompilerParams(collective_id=0, has_side_effects=True),
     )(src, cnt, x, down, up, ang)

time: 115 us -> 114 us (level)
  no operation moved by 1% of the time
where the time goes in v6:
time: 114 us
  Pallas kernels  113 us (99%)
    pallas_call x1, Pallas kernels, front(): pl.pallas_call(front_kernel, name='front', in_specs=[smem, smem, anywhere...  47.8 us
    pallas_call x1, Pallas kernels, back(): pl.pallas_call(back_kernel, name='back', in_specs=[inside] * 4 + [pl.Bloc...  38.7 us
    pallas_call x1, Pallas kernels, layer(): pl.pallas_call(layer_kernel, name='layer', grid=(LAYER_TILES,), in_specs=...  21.3 us
    pallas_call x1, Pallas kernels, last(): pl.pallas_call(last_kernel, name='last', grid=(LAST_TILES,), in_specs=[wi...  5.33 us

profile of v6, /device:TPU:1, one launch (start us, length us, event | category | flops | bytes accessed | tf_op | source)
XLA Modules:
  0.0 113.7 jit_solution(16600634802969144328)
XLA Ops:
  0.6 47.8 %front.1 = (bf16[1024,128]{1,0:T(8,128)(2,1)}, f32[1024,128]{1,0:T(8,128)}, bf16[2048,512]{1,0:T(8,128)(2,1)}, bf16[2048,512]{1,0:T(8,128)(2,1)}, bf16[2048,512]{1,0:T(8,128)(2,1)}) custom-call(s32[8,32]{1,0:T(8,128)} %bitcast.12, s32[32]{0:T(128)} %cnt.1, bf16[2048,512]{1,0:T(8,128)(2,1)} %x.3, bf16[64,512]{1,0:T(8,128)(2,1)} %bitcast.8, ...), custom_call_target="tpu_custom_call" | custom-call | tf_op jit(solution)/shard_map/front/pallas_call | solution.py:313
  48.4 21.3 %layer.1 = (bf16[2048,512]{1,0:T(8,128)(2,1)}, bf16[2048,512]{1,0:T(8,128)(2,1)}, bf16[1024,128]{1,0:T(8,128)(2,1)}, f32[2048,128]{1,0:T(8,128)}) custom-call(bf16[2048,512]{1,0:T(8,128)(2,1)} %x.3, bf16[2048,512]{1,0:T(8,128)(2,1)} %cot.1, bf16[2048,512]{1,0:T(8,128)(2,1)} %get-tuple-element.13.ups, bf16[2048,512]{1,0:T(8,128)(2,1)} %get-tuple-element.14.slopes, ...), custom_call_target="tpu_custom_call" | custom-call | tf_op jit(solution)/shard_map/layer/pallas_call | solution.py:406
  69.7 38.7 %back.1.total = f32[1024,128]{1,0:T(8,128)} custom-call(s32[8,32]{1,0:T(8,128)} %bitcast.13, s32[1,32]{1,0:T(1,128)} %bitcast.14, s32[16,128]{1,0:T(8,128)} %bitcast.11, bf16[1024,128]{1,0:T(8,128)(2,1)} %get-tuple-element.17.got, f32[2048,128]{1,0:T(8,128)} %get-tuple-element.18.gown_in, bf16[2048,512]{1,0:T(8,128)(2,1)} %get-tuple-element.19.amat_in), custom_call_target="tpu_custom_call" | custom-call | tf_op jit(solution)/shard_map/back/pallas_call | solution.py:598
  108.4 5.3 %last.1 = (bf16[2048,512]{1,0:T(8,128)(2,1)}, bf16[2048,512]{1,0:T(8,128)(2,1)}) custom-call(bf16[2048,512]{1,0:T(8,128)(2,1)} %get-tuple-element.16.gmsg, f32[1024,128]{1,0:T(8,128)} %back.1.total, f32[1024,128]{1,0:T(8,128)} %get-tuple-element.20.pre, bf16[64,512]{1,0:T(8,128)(2,1)} %bitcast.9, bf16[2048,512]{1,0:T(8,128)(2,1)} %get-tuple-element.21.res), custom_call_target="tpu_custom_call" | custom-call | tf_op jit(solution)/shard_map/last/pallas_call | solution.py:643
